TPU v7x, 32 devices: a whole 2x2x4 slice. The times are simulated.
32 devices in a mesh: groups: 1, ep: 16 (over z, y, x), side: 2 (over core).
Axes of the slice: x: 2, y: 2, z: 4, core: 2. Of those that a mesh axis runs over, the one named last changes fastest.
Arguments:
- queries: bfloat16 [128, 128, 576], P(('groups', 'ep', 'side')), may hold values from -16 to 16
- latent_cache: bfloat16 [64, 128, 576], P(('groups', 'ep', 'side')), may hold values from -16 to 16
- new_latent: bfloat16 [128, 576], P(('groups', 'ep', 'side')), may hold values from -6 to 6
- lengths: int32 [64], P(('groups', 'ep', 'side')), may hold values from 2 to 128
- residual: bfloat16 [128, 3584], P(('groups', 'ep', 'side')), may hold values from -6 to 6
- norm_gain: float32 [3584], replicated, may hold values from 0.5 to 1.5
- value_up: bfloat16 [128, 512, 128], P(('ep', 'side')), may hold values from -0.25 to 0.25
- output_proj: bfloat16 [128, 128, 3584], P(('ep', 'side')), may hold values from -0.1875 to 0.1875
- expert_ids: int32 [128, 8], P(('groups', 'ep', 'side')), may hold values from 0 to 15, all different within a row; in each aligned block of 4 rows (0 to 3, 4 to 7, ...) at most 2 rows name the same one
- expert_weights: float32 [128, 8], P(('groups', 'ep', 'side')), may hold values from 0.05 to 0.4
- gate_proj: bfloat16 [16, 3584, 1024], P('ep', None, 'side'), may hold values from -0.09375 to 0.09375
- up_proj: bfloat16 [16, 3584, 1024], P('ep', None, 'side'), may hold values from -0.09375 to 0.09375
- down_proj: bfloat16 [16, 1024, 3584], P('ep', 'side'), may hold values from -0.1875 to 0.1875
Outputs:
- layer_out: bfloat16 [128, 3584], P(('groups', 'ep', 'side'))
Inputs may be any that keep to these rules, and one draw needn't show every extreme that they name: `expert_ids`: each row names 8 different experts. The 4 rows of one device name any one expert at most 2 times, and in every draw some device's rows name some expert exactly 2 times.
All inputs are finite; a program needn't handle non-finite values.
Results may differ from a plain program's by a relative error of at most 0.0056.
Values may be sent and summed in bfloat16 or wider, within the bound.
No kernel may reach another device: no remote copies, remote signals or barrier semaphores. Data moves between devices by JAX's collectives and lax.ppermute only.
A program may use at most 64 MiB of HBM per device.

v0:
```python
import jax
import jax.numpy as jnp
from jax import lax
from jax.sharding import PartitionSpec as P

LAT = 512
QKD = 192


norm_epsilon = 1e-06
masked_score = -1e30


def attend_block(query_steps, latent_cache, new_steps, lengths):
    factor = 1.0 / QKD**0.5
    cache_scores = (
        jnp.einsum("rshk,rpk->rshp", query_steps, latent_cache, preferred_element_type=jnp.float32)
        * factor
    )
    fresh_scores = (
        jnp.einsum("rshk,rqk->rshq", query_steps, new_steps, preferred_element_type=jnp.float32)
        * factor
    )
    cache_live = (
        lax.broadcasted_iota(jnp.int32, cache_scores.shape, 3) < lengths[:, None, None, None]
    )
    fresh_live = lax.broadcasted_iota(jnp.int32, fresh_scores.shape, 3) <= lax.broadcasted_iota(
        jnp.int32, fresh_scores.shape, 1
    )
    cache_scores = jnp.where(cache_live, cache_scores, masked_score)
    fresh_scores = jnp.where(fresh_live, fresh_scores, masked_score)
    highest_score = jnp.maximum(jnp.max(cache_scores, axis=3), jnp.max(fresh_scores, axis=3))[
        ..., None
    ]
    cache_weight = jnp.where(cache_live, jnp.exp(cache_scores - highest_score), 0.0)
    fresh_weight = jnp.where(fresh_live, jnp.exp(fresh_scores - highest_score), 0.0)
    weight_sum = jnp.sum(cache_weight, axis=3) + jnp.sum(fresh_weight, axis=3)
    merged = jnp.einsum(
        "rshp,rpl->rshl",
        cache_weight.astype(jnp.bfloat16),
        latent_cache[:, :, :LAT],
        preferred_element_type=jnp.float32,
    )
    merged = merged + jnp.einsum(
        "rshq,rql->rshl",
        fresh_weight.astype(jnp.bfloat16),
        new_steps[:, :, :LAT],
        preferred_element_type=jnp.float32,
    )
    return (merged / weight_sum[..., None]).astype(jnp.bfloat16)


def local(
    queries,
    latent_cache,
    new_latent,
    lengths,
    residual,
    norm_gain,
    value_up,
    output_proj,
    expert_ids,
    expert_weights,
    gate_proj,
    up_proj,
    down_proj,
):
    requests = latent_cache.shape[0]
    positions = queries.shape[0] // requests
    head_count = queries.shape[1]
    feature = residual.shape[1]
    query_steps = queries.reshape(requests, positions, head_count, queries.shape[2])
    new_steps = new_latent.reshape(requests, positions, new_latent.shape[1])
    resid_steps = residual.reshape(requests, positions, feature)
    chosen_steps = expert_ids.reshape(requests, positions, expert_ids.shape[1])
    weight_steps = expert_weights.reshape(requests, positions, expert_weights.shape[1])
    expert_count = lax.axis_size("ep")
    side_count = lax.axis_size("side")
    full_rows = requests * positions
    capacity = min(
        full_rows, max(2, (full_rows * expert_ids.shape[1] + expert_count - 1) // expert_count)
    )
    uv_used, out_used = (
        lax.all_gather(value_up, "side", axis=0, tiled=True),
        lax.all_gather(output_proj, "side", axis=0, tiled=True),
    )
    flat_out = out_used.reshape(out_used.shape[0] * out_used.shape[1], feature)
    row_count = requests * positions
    latent = attend_block(query_steps, latent_cache, new_steps, lengths)
    latent = latent.reshape(row_count, head_count, latent.shape[3])
    arrived = lax.all_to_all(latent, "ep", split_axis=1, concat_axis=0, tiled=True)
    head_out = jnp.einsum(
        "ngl,glv->ngv", arrived, uv_used, preferred_element_type=jnp.float32
    ).astype(jnp.bfloat16)
    head_flat = head_out.reshape(head_out.shape[0], head_out.shape[1] * head_out.shape[2])
    attention = lax.psum_scatter(
        jnp.dot(head_flat, flat_out, preferred_element_type=jnp.float32),
        "ep",
        scatter_dimension=0,
        tiled=True,
    )
    resid_rows = resid_steps.reshape(row_count, feature)
    stream = resid_rows.astype(jnp.float32) + attention
    mean_square = jnp.mean(stream * stream, axis=1, keepdims=True)
    normed = (stream * lax.rsqrt(mean_square + norm_epsilon) * norm_gain[None, :]).astype(
        jnp.bfloat16
    )
    chosen_rows = chosen_steps.reshape(row_count, chosen_steps.shape[2])
    weight_rows = weight_steps.reshape(row_count, weight_steps.shape[2])
    chosen = chosen_rows[:, :, None] == lax.broadcasted_iota(jnp.int32, (1, 1, expert_count), 2)
    picked_count = jnp.sum(chosen.astype(jnp.int32), axis=1)
    routed_share = jnp.sum(jnp.where(chosen, weight_rows[:, :, None], 0.0), axis=1)
    before = jnp.cumsum(picked_count, axis=0) - picked_count
    placement = (before[:, :, None] == lax.broadcasted_iota(jnp.int32, (1, 1, capacity), 2)) & (
        picked_count[:, :, None] > 0
    )
    outbound = jnp.einsum(
        "nec,nd->ecd", placement.astype(jnp.bfloat16), normed, preferred_element_type=jnp.float32
    ).astype(jnp.bfloat16)
    outbound = jnp.broadcast_to(
        outbound[:, None], (expert_count, side_count, capacity, feature)
    ).reshape(expert_count * side_count, capacity, feature)
    arrived_rows = lax.all_to_all(outbound, ("ep", "side"), split_axis=0, concat_axis=0, tiled=True)
    source_total, item_total, width_total = arrived_rows.shape
    flat_rows = arrived_rows.reshape(source_total * item_total, width_total)
    gate_part = jnp.dot(flat_rows, gate_proj[0], preferred_element_type=jnp.float32)
    up_part = jnp.dot(flat_rows, up_proj[0], preferred_element_type=jnp.float32)
    hidden = (jax.nn.silu(gate_part) * up_part).astype(jnp.bfloat16)
    partial_value = jnp.dot(hidden, down_proj[0], preferred_element_type=jnp.float32).astype(
        jnp.bfloat16
    )
    partial_out = partial_value.reshape(source_total, item_total, width_total)
    returned = lax.all_to_all(partial_out, ("ep", "side"), split_axis=0, concat_axis=0, tiled=True)
    halves = returned.reshape(expert_count, side_count, capacity, feature).astype(jnp.float32)
    summed = jnp.sum(halves, axis=1)
    coefficient = jnp.where(placement, routed_share[:, :, None], 0.0)
    mixture = jnp.einsum("nec,ecd->nd", coefficient, summed, precision=lax.Precision.HIGHEST)
    output_rows = (stream + mixture).astype(jnp.bfloat16)
    output = output_rows.reshape(requests, positions, feature)
    return output.reshape(requests * positions, feature)


def solution(mesh):
    in_specs = (
        P(("groups", "ep", "side"), None, None),
        P(("groups", "ep", "side"), None, None),
        P(("groups", "ep", "side"), None),
        P(("groups", "ep", "side")),
        P(("groups", "ep", "side"), None),
        P(),
        P(("ep", "side"), None, None),
        P(("ep", "side"), None, None),
        P(("groups", "ep", "side"), None),
        P(("groups", "ep", "side"), None),
        P("ep", None, "side"),
        P("ep", None, "side"),
        P("ep", "side", None),
    )
    out_specs = P(("groups", "ep", "side"), None)
    return jax.shard_map(local, mesh=mesh, in_specs=in_specs, out_specs=out_specs, check_vma=False)
```

profile of v0, /device:TPU:0, one launch (start us, length us, event | category | flops | bytes accessed | tf_op | source)
XLA Modules:
  0.0 215.8 jit_solution(1367729353984791587)
XLA Ops:
  6.5 0.0 all-gather.3.cloned.1.call-start
  6.6 0.7 all-gather.3.cloned.1.call-update
  7.3 0.0 all-gather.5.cloned.1.call-start
  7.3 0.7 all-gather.5.cloned.1.call-update
  8.0 0.0 all-reduce.3.cloned.1.call-start
  8.1 0.2 fusion.61
  8.4 0.3 fusion.60
  8.7 0.1 fusion.27
  8.8 0.4 fusion.24
  9.3 0.4 fusion.8
  9.6 0.4 copy.35
  10.0 23.2 %all_to_all.28 = bf16[4,128,512]{2,0,1:T(4,128)(2,1)S(1)} all-to-all(bf16[4,128,512]{2,0,1:T(4,128)(2,1)S(1)} %copy.35), channel_id=1, replica_groups=mesh['groups'=1,'ep'=16,'side'=2] {'ep'}, dimensions={1} | all-to-all | bytes 1048576 | tf_op jit(solution)/shard_map/all_to_all | solution.py:91
  33.3 0.1 copy.53
  33.4 8.3 %all-gather.5.cloned.1.call-done = bf16[8,128,3584]{2,1,0:T(8,128)(2,1)} async-done(((bf16[4,128,3584]{2,1,0:T(8,128)(2,1)}), bf16[8,128,3584]{2,1,0:T(8,128)(2,1)}) %all-gather.5.cloned.1.call-update) | async-done | bytes 7340048 | tf_op jit(solution)/shard_map/all_gather | solution.py:85
  41.7 6.1 %convolution_bitcast_fusion = f32[64,3584]{1,0:T(8,128)} fusion(bf16[8,128,3584]{2,1,0:T(8,128)(2,1)} %all-gather.5.cloned.1.call-done, bf16[8,512,128]{2,1,0:T(8,128)(2,1)} %all-gather.3.cloned.1.call-done, bf16[64,8,512]{2,1,0:T(8,128)(2,1)S(1)} %bitcast.74), kind=kOutput, calls=%fused_computation | convolution fusion | flops 536936448 | bytes 9830400 | tf_op jit(solution)/shard_map/dot_general | solution.py:97
  47.9 0.1 convert_reduce_fusion.1
  48.0 0.6 dynamic-slice
  49.2 111.4 %all-reduce.3.cloned.1.call-done = f32[64,3584]{1,0:T(8,128)} async-done(((f32[64,3584]{1,0:T(8,128)}), f32[64,3584]{1,0:T(8,128)}) %all-reduce.3.cloned.1.call-update) | async-done | bytes 917520
  160.7 1.0 multiply_reduce_fusion
  161.7 1.2 convolution_convert_fusion.1
  162.9 0.2 copy.39
  163.1 0.2 broadcast_in_dim.60
  163.4 17.7 %all_to_all.29 = bf16[32,2,3584]{2,1,0:T(2,128)(2,1)S(1)} all-to-all(bf16[32,2,3584]{2,1,0:T(2,128)(2,1)S(1)} %bitcast.76), channel_id=1, replica_groups=mesh['groups'=1,'ep'=16,'side'=2] {'ep','side'}, dimensions={0} | all-to-all | bytes 917504 | tf_op jit(solution)/shard_map/all_to_all | solution.py:123
  181.1 0.2 reshape.64
  181.3 2.8 %fusion.5 = f32[64,512]{1,0:T(8,128)S(1)} fusion(bf16[64,3584]{1,0:T(8,128)(2,1)S(1)} %reshape.64, bf16[1,3584,512]{2,1,0:T(8,128)(2,1)} %param.23), kind=kOutput, calls=%fused_computation.9 | convolution fusion | flops 234881024 | bytes 4259840 | tf_op jit(solution)/shard_map/dot_general | solution.py:126
  184.1 4.6 %convolution_convert_fusion = bf16[64,3584]{1,0:T(8,128)(2,1)S(1)} fusion(bf16[1,512,3584]{2,1,0:T(8,128)(2,1)} %param.25, bf16[64,3584]{1,0:T(8,128)(2,1)S(1)} %reshape.64, bf16[1,3584,512]{2,1,0:T(8,128)(2,1)} %param.24, f32[64,512]{1,0:T(8,128)S(1)} %fusion.5), kind=kOutput, calls=%fused_computation.1 | convolution fusion | flops 470188032 | bytes 8388608 | tf_op jit(solution)/shard_map/dot_general | solution.py:129
  188.7 0.9 reshape.65
  189.7 2.8 %all-to-all-start.2 = ((bf16[32,2,3584]{2,1,0:T(2,128)(2,1)}), bf16[32,2,3584]{2,1,0:T(2,128)(2,1)S(1)}, u32[]{:S(2)}, u32[]{:S(2)}) async-start(bf16[32,2,3584]{2,1,0:T(2,128)(2,1)} %reshape.65), calls=%async_computation.2 | async-start | bytes 917504 | tf_op jit(solution)/shard_map/all_to_all | solution.py:133
  192.5 0.1 select_reduce_fusion
  192.5 14.3 %all-to-all-done.2 = bf16[32,2,3584]{2,1,0:T(2,128)(2,1)S(1)} async-done(((bf16[32,2,3584]{2,1,0:T(2,128)(2,1)}), bf16[32,2,3584]{2,1,0:T(2,128)(2,1)S(1)}, u32[]{:S(2)}, u32[]{:S(2)}) %all-to-all-start.2) | async-done | bytes 458784 | tf_op jit(solution)/shard_map/all_to_all | solution.py:133
  206.9 0.5 convert_reduce_fusion
  207.4 1.9 fusion.1
  (30 shorter events, 0.3 us)
Async XLA Ops:
  6.5 1.6 copy-start
  6.5 1.5 copy-start.3
  6.5 1.8 copy-start.1
  6.5 1.8 copy-start.6
  6.5 26.9 %all-gather.3.cloned.1.call-start = ((), (), s32[]{:S(2)}) async-start(), calls=%async_computation.3 | async-start | bytes 1572864 | tf_op jit(solution)/shard_map/all_gather | solution.py:84
  7.3 34.5 %all-gather.5.cloned.1.call-start = ((), (), s32[]{:S(2)}) async-start(), calls=%async_computation.4 | async-start | bytes 11010048 | tf_op jit(solution)/shard_map/all_gather | solution.py:85
  8.0 152.6 %all-reduce.3.cloned.1.call-start = ((), (), s32[]{:S(2)}) async-start(), calls=%async_computation.5 | async-start | bytes 1835008
  41.7 6.1 %copy-start.5 = (s32[4,8]{1,0:T(4,128)S(1)}, s32[4,8]{1,0:T(4,128)}, u32[]{:S(2)}) copy-start(s32[4,8]{1,0:T(4,128)} %param.21) | copy-start | bytes 388
  41.7 6.3 %copy-start.8 = (u32[32]{0:T(128)S(1)}, u32[32]{0:T(128)}, u32[]{:S(2)}) copy-start(u32[32]{0:T(128)} %constant.37) | copy-start | bytes 388
  41.7 118.9 %copy-start.2 = (bf16[4,3584]{1,0:T(4,128)(2,1)S(1)}, bf16[4,3584]{1,0:T(4,128)(2,1)}, u32[]{:S(2)}) copy-start(bf16[4,3584]{1,0:T(4,128)(2,1)} %param.17) | copy-start | bytes 86020
  41.7 120.0 %copy-start.4 = (f32[3584]{0:T(1024)S(1)}, f32[3584]{0:T(1024)}, u32[]{:S(2)}) copy-start(f32[3584]{0:T(1024)} %param.18) | copy-start | bytes 43012
  184.1 8.4 %copy-start.7 = (f32[4,8]{1,0:T(4,128)S(1)}, f32[4,8]{1,0:T(4,128)}, u32[]{:S(2)}) copy-start(f32[4,8]{1,0:T(4,128)} %param.22) | copy-start | bytes 388
  189.7 17.2 %all-to-all-start.2 = ((bf16[32,2,3584]{2,1,0:T(2,128)(2,1)}), bf16[32,2,3584]{2,1,0:T(2,128)(2,1)S(1)}, u32[]{:S(2)}, u32[]{:S(2)}) async-start(bf16[32,2,3584]{2,1,0:T(2,128)(2,1)} %reshape.65), calls=%async_computation.2 | async-start | bytes 917504 | tf_op jit(solution)/shard_map/all_to_all | solution.py:133
Sparse Core Ops, SparseCore 0:
  8.9 11.7 all-gather.2
  22.2 19.4 all-gather.4
  48.0 112.6 all-reduce.2
where the time goes:
time: 216 us
  waiting for transfers between devices  135 us (62%)
  blocking collectives  41 us (19%)
  matrix products  17.9 us (8%)
  between operations  14 us (6%)
  starting transfers between devices  2.87 us (1%)
  local copies, waits for them, and re-layouts  2.8 us (1%)
    unnamed x4, waiting for transfers between devices  113 us
    all_to_all x1, blocking collectives, local(): lax.all_to_all(latent, 'ep', split_axis=1, concat_axis=0, tiled=True)  23.2 us
    all_to_all x1, blocking collectives, local(): lax.all_to_all(outbound, ('ep', 'side'), split_axis=0, concat_axis=0, til...  17.7 us
    all_to_all x1, waiting for transfers between devices, local(): lax.all_to_all(partial_out, ('ep', 'side'), split_axis=0, concat_axis=0,...  14.3 us
    all_gather x1, waiting for transfers between devices, local(): lax.all_gather(output_proj, 'side', axis=0, tiled=True)  8.29 us
    dot_general x1, matrix products, local(): jnp.dot(head_flat, flat_out, preferred_element_type=jnp.float32)  6.09 us
    dot_general x1, matrix products, local(): jnp.dot(hidden, down_proj[0], preferred_element_type=jnp.float32)  4.62 us
  transfers between devices with their start and end apart: 4, of which 3 were waited for; matrix products, arithmetic and copies ran while one was open for 1% of the time, Pallas kernels for 0%

commit v1 on v0

v1 whole, which is shorter than its diff:
```python
import jax
import jax.numpy as jnp
from jax import lax
from jax.sharding import PartitionSpec as P

LAT = 512
QKD = 192


norm_epsilon = 1e-06
masked_score = -1e30


def attend_block(query_steps, latent_cache, new_steps, lengths):
    factor = 1.0 / QKD**0.5
    cache_scores = (
        jnp.einsum("rshk,rpk->rshp", query_steps, latent_cache, preferred_element_type=jnp.float32)
        * factor
    )
    fresh_scores = (
        jnp.einsum("rshk,rqk->rshq", query_steps, new_steps, preferred_element_type=jnp.float32)
        * factor
    )
    cache_live = (
        lax.broadcasted_iota(jnp.int32, cache_scores.shape, 3) < lengths[:, None, None, None]
    )
    fresh_live = lax.broadcasted_iota(jnp.int32, fresh_scores.shape, 3) <= lax.broadcasted_iota(
        jnp.int32, fresh_scores.shape, 1
    )
    cache_scores = jnp.where(cache_live, cache_scores, masked_score)
    fresh_scores = jnp.where(fresh_live, fresh_scores, masked_score)
    highest_score = jnp.maximum(jnp.max(cache_scores, axis=3), jnp.max(fresh_scores, axis=3))[
        ..., None
    ]
    cache_weight = jnp.where(cache_live, jnp.exp(cache_scores - highest_score), 0.0)
    fresh_weight = jnp.where(fresh_live, jnp.exp(fresh_scores - highest_score), 0.0)
    weight_sum = jnp.sum(cache_weight, axis=3) + jnp.sum(fresh_weight, axis=3)
    merged = jnp.einsum(
        "rshp,rpl->rshl",
        cache_weight.astype(jnp.bfloat16),
        latent_cache[:, :, :LAT],
        preferred_element_type=jnp.float32,
    )
    merged = merged + jnp.einsum(
        "rshq,rql->rshl",
        fresh_weight.astype(jnp.bfloat16),
        new_steps[:, :, :LAT],
        preferred_element_type=jnp.float32,
    )
    return (merged / weight_sum[..., None]).astype(jnp.bfloat16)


def swap_sides(block, shift):
    count = lax.axis_size("side")
    return lax.ppermute(block, "side", [(s, (s + shift) % count) for s in range(count)])


def local(
    queries,
    latent_cache,
    new_latent,
    lengths,
    residual,
    norm_gain,
    value_up,
    output_proj,
    expert_ids,
    expert_weights,
    gate_proj,
    up_proj,
    down_proj,
):
    requests = latent_cache.shape[0]
    positions = queries.shape[0] // requests
    head_count = queries.shape[1]
    feature = residual.shape[1]
    row_count = requests * positions
    ep_count = lax.axis_size("ep")
    side_count = lax.axis_size("side")
    side = lax.axis_index("side")
    own_heads = value_up.shape[0]
    capacity = min(
        row_count, max(2, (row_count * expert_ids.shape[1] + ep_count - 1) // ep_count)
    )
    query_steps = queries.reshape(requests, positions, head_count, queries.shape[2])
    new_steps = new_latent.reshape(requests, positions, new_latent.shape[1])
    flat_out = output_proj.reshape(own_heads * output_proj.shape[1], feature)

    latent = attend_block(query_steps, latent_cache, new_steps, lengths)
    latent = latent.reshape(row_count, head_count, latent.shape[3])
    arrived = lax.all_to_all(latent, ("ep", "side"), split_axis=1, concat_axis=0, tiled=True)
    head_out = jnp.einsum(
        "ngl,glv->ngv", arrived, value_up, preferred_element_type=jnp.float32
    ).astype(jnp.bfloat16)
    head_flat = head_out.reshape(
        ep_count, side_count, row_count, own_heads * head_out.shape[2]
    )

    def project(shift):
        rows = lax.dynamic_index_in_dim(
            head_flat, (side + shift) % side_count, axis=1, keepdims=False
        ).reshape(ep_count * row_count, head_flat.shape[3])
        return jnp.dot(rows, flat_out, preferred_element_type=jnp.float32)

    others = [
        swap_sides(project(shift).astype(jnp.bfloat16), shift) for shift in range(1, side_count)
    ]
    contribution = project(0)
    for other in others:
        contribution = contribution + other.astype(jnp.float32)
    shared = lax.all_to_all(
        contribution.astype(jnp.bfloat16).reshape(ep_count, row_count, feature),
        "ep",
        split_axis=0,
        concat_axis=0,
        tiled=True,
    )
    attention = jnp.sum(shared.astype(jnp.float32), axis=0)
    stream = residual.astype(jnp.float32) + attention
    mean_square = jnp.mean(stream * stream, axis=1, keepdims=True)
    normed = (stream * lax.rsqrt(mean_square + norm_epsilon) * norm_gain[None, :]).astype(
        jnp.bfloat16
    )
    chosen = expert_ids[:, :, None] == lax.broadcasted_iota(jnp.int32, (1, 1, ep_count), 2)
    picked_count = jnp.sum(chosen.astype(jnp.int32), axis=1)
    routed_share = jnp.sum(jnp.where(chosen, expert_weights[:, :, None], 0.0), axis=1)
    before = jnp.cumsum(picked_count, axis=0) - picked_count
    placement = (before[:, :, None] == lax.broadcasted_iota(jnp.int32, (1, 1, capacity), 2)) & (
        picked_count[:, :, None] > 0
    )
    outbound = jnp.einsum(
        "nec,nd->ecd", placement.astype(jnp.bfloat16), normed, preferred_element_type=jnp.float32
    ).astype(jnp.bfloat16)
    own_rows = lax.all_to_all(outbound, "ep", split_axis=0, concat_axis=0, tiled=True).reshape(
        ep_count * capacity, feature
    )
    flat_rows = jnp.concatenate(
        [own_rows] + [swap_sides(own_rows, side_count - shift) for shift in range(1, side_count)]
    )
    gate_part = jnp.dot(flat_rows, gate_proj[0], preferred_element_type=jnp.float32)
    up_part = jnp.dot(flat_rows, up_proj[0], preferred_element_type=jnp.float32)
    hidden = (jax.nn.silu(gate_part) * up_part).astype(jnp.bfloat16)
    partial_value = jnp.dot(hidden, down_proj[0], preferred_element_type=jnp.float32).astype(
        jnp.bfloat16
    )
    partial_value = partial_value.reshape(side_count, ep_count * capacity, feature)
    both = partial_value[0].astype(jnp.float32)
    for shift in range(1, side_count):
        both = both + swap_sides(partial_value[shift], shift).astype(jnp.float32)
    returned = lax.all_to_all(
        both.astype(jnp.bfloat16).reshape(ep_count, capacity, feature),
        "ep",
        split_axis=0,
        concat_axis=0,
        tiled=True,
    )
    coefficient = jnp.where(placement, routed_share[:, :, None], 0.0)
    mixture = jnp.einsum(
        "nec,ecd->nd",
        coefficient,
        returned.astype(jnp.float32),
        precision=lax.Precision.HIGHEST,
    )
    return (stream + mixture).astype(jnp.bfloat16)


def solution(mesh):
    in_specs = (
        P(("groups", "ep", "side"), None, None),
        P(("groups", "ep", "side"), None, None),
        P(("groups", "ep", "side"), None),
        P(("groups", "ep", "side")),
        P(("groups", "ep", "side"), None),
        P(),
        P(("ep", "side"), None, None),
        P(("ep", "side"), None, None),
        P(("groups", "ep", "side"), None),
        P(("groups", "ep", "side"), None),
        P("ep", None, "side"),
        P("ep", None, "side"),
        P("ep", "side", None),
    )
    out_specs = P(("groups", "ep", "side"), None)
    return jax.shard_map(local, mesh=mesh, in_specs=in_specs, out_specs=out_specs, check_vma=False)
```

time: 216 us -> 96.6 us (0.45)
  waiting for transfers between devices: 135 us -> 43.7 us
  blocking collectives: 41 us -> 11.9 us
  between operations: 14 us -> 0.3 us
  starting transfers between devices: 2.87 us -> 15.4 us
  local copies, waits for them, and re-layouts: 2.8 us -> 5.6 us
    unnamed x4 -> x0, waiting for transfers between devices: 113 us -> none
    all_to_all x2 -> x1, blocking collectives: 41 us -> 11.9 us  [local(): lax.all_to_all(outbound, 'ep', split_axis=0, concat_axis=0, tiled=True)]
    all_to_all x1 -> x3, waiting for transfers between devices: 14.3 us -> 39.1 us  [the longest x1 15.6 us: local(): lax.all_to_all(latent, ('ep', 'side'), split_axis=1, concat_axis=0, tiled...]
    all_to_all x1 -> x3, starting transfers between devices: 2.76 us -> 15 us  [the longest x1 7.32 us: local(): lax.all_to_all(latent, ('ep', 'side'), split_axis=1, concat_axis=0, tiled...]
    all_gather x2 -> x0, waiting for transfers between devices: 8.31 us -> none  [the longest x1 8.29 us: local(): lax.all_gather(output_proj, 'side', axis=0, tiled=True)]
    ppermute x0 -> x3, waiting for transfers between devices: none -> 4.58 us  [swap_sides(): lax.ppermute(block, 'side', [(s, (s + shift) % count) for s in range(coun...]
    dot_general x3 -> x5, matrix products: 10.8 us -> 9.53 us  [the longest x2 5.57 us: project(): return jnp.dot(rows, flat_out, preferred_element_type=jnp.float32)]
  transfers between devices with their start and end apart: 4 -> 6, of which waited for: 3 -> 6; matrix products, arithmetic and copies ran while one was open for 1% -> 0% of each run, Pallas kernels for 0% -> 0%
where the time goes in v1:
time: 96.6 us; the launch traced here: 95.9 us
  waiting for transfers between devices  43.7 us (45%)
  matrix products  17.7 us (18%)
  starting transfers between devices  15.4 us (16%)
  blocking collectives  11.9 us (12%)
  local copies, waits for them, and re-layouts  5.6 us (6%)
  other arithmetic  1.43 us (1%)
    all_to_all x1, waiting for transfers between devices, local(): lax.all_to_all(latent, ('ep', 'side'), split_axis=1, concat_axis=0, tiled...  15.6 us
    all_to_all x1, waiting for transfers between devices, local(): lax.all_to_all(contribution.astype(jnp.bfloat16).reshape(ep_count, row_co...  14 us
    all_to_all x1, blocking collectives, local(): lax.all_to_all(outbound, 'ep', split_axis=0, concat_axis=0, tiled=True)  11.9 us
    all_to_all x1, waiting for transfers between devices, local(): lax.all_to_all(both.astype(jnp.bfloat16).reshape(ep_count, capacity, feat...  9.48 us
    all_to_all x1, starting transfers between devices, local(): lax.all_to_all(latent, ('ep', 'side'), split_axis=1, concat_axis=0, tiled...  7.32 us
    dot_general x2, matrix products, project(): return jnp.dot(rows, flat_out, preferred_element_type=jnp.float32)  5.57 us
    dot_general x1, matrix products, local(): jnp.dot(hidden, down_proj[0], preferred_element_type=jnp.float32)  4.63 us
    ppermute x3, waiting for transfers between devices, swap_sides(): lax.ppermute(block, 'side', [(s, (s + shift) % count) for s in range(coun...  4.58 us
  transfers between devices with their start and end apart: 6, of which 6 were waited for; matrix products, arithmetic and copies ran while one was open for 0% of the time, Pallas kernels for 0%

profile of v1, /device:TPU:0, one launch (start us, length us, event | category | flops | bytes accessed | tf_op | source)
XLA Modules:
  0.0 95.9 jit_solution(3157775630711031457)
XLA Ops:
  0.0 0.8 reshape.84
  0.8 0.3 copy-done
  1.1 0.2 fusion.49
  1.3 1.3 %fusion.48 = (f32[2,2,128]{2,1,0:T(2,128)S(1)}, f32[2,2,128,128]{2,3,1,0:T(8,128)S(1)}) fusion(bf16[2,2,128,576]{2,3,1,0:T(8,128)(2,1)S(1)} %bitcast.66, bf16[2,128,576]{1,2,0:T(8,128)(2,1)} %param.14, s32[2]{0:T(128)} %param.16), kind=kOutput, calls=%fused_computation.71 | convolution fusion | flops 75759104 | bytes 1148936 | tf_op jit(solution)/shard_map/rshk,rpk->rshp/dot_general | solution.py:17
  2.6 1.4 %fusion.13 = f32[2,2,128,512]{3,2,1,0:T(8,128)S(1)} fusion(bf16[2,128,576]{1,2,0:T(8,128)(2,1)} %param.14, f32[2,2,128,128]{2,3,1,0:T(8,128)S(1)} %get-tuple-element.8, f32[2,2,128]{2,1,0:T(2,128)S(1)} %max.7, s32[2]{0:T(128)} %param.16), kind=kOutput, calls=%fused_computation.25 | convolution fusion | flops 67371008 | bytes 1575424 | tf_op jit(solution)/shard_map/rshp,rpl->rshl/dot_general | solution.py:38
  4.0 0.8 fusion.17
  4.7 0.7 reshape.74
  5.5 0.4 fusion.8
  5.9 1.2 %copy.33 = bf16[4,128,512]{2,0,1:T(4,128)(2,1)} copy(bf16[4,128,512]{2,1,0:T(8,128)(2,1)S(1)} %bitcast.72) | data formatting | bytes 1048576 | tf_op jit(solution)/shard_map/reshape | solution.py:90
  7.1 7.3 %all-to-all-start = ((bf16[4,128,512]{2,0,1:T(4,128)(2,1)}), bf16[4,128,512]{2,0,1:T(4,128)(2,1)S(1)}, u32[]{:S(2)}, u32[]{:S(2)}) async-start(bf16[4,128,512]{2,0,1:T(4,128)(2,1)} %copy.33), calls=%async_computation | async-start | bytes 1048576 | tf_op jit(solution)/shard_map/all_to_all | solution.py:91
  14.4 15.6 %all-to-all-done = bf16[4,128,512]{2,0,1:T(4,128)(2,1)S(1)} async-done(((bf16[4,128,512]{2,0,1:T(4,128)(2,1)}), bf16[4,128,512]{2,0,1:T(4,128)(2,1)S(1)}, u32[]{:S(2)}, u32[]{:S(2)}) %all-to-all-start) | async-done | bytes 524320 | tf_op jit(solution)/shard_map/all_to_all | solution.py:91
  30.0 0.2 copy.47
  30.3 0.3 fusion.10
  30.9 2.8 %convolution_convert_fusion.1 = bf16[64,3584]{1,0:T(8,128)(2,1)S(1)} fusion(bf16[64,512]{1,0:T(8,128)(2,1)S(1)} %reshape.79, bf16[512,3584]{1,0:T(8,128)(2,1)} %bitcast.68), kind=kOutput, calls=%fused_computation.1 | convolution fusion | flops 235110400 | bytes 4194304 | tf_op jit(solution)/shard_map/dot_general | solution.py:103
  33.8 1.8 %collective-permute-done = bf16[64,3584]{1,0:T(8,128)(2,1)S(1)} collective-permute-done((bf16[64,3584]{1,0:T(8,128)(2,1)S(1)}, bf16[64,3584]{1,0:T(8,128)(2,1)S(1)}, u32[]{:S(2)}, u32[]{:S(2)}) %collective-permute-start) | collective-permute-done | bytes 458784 | tf_op jit(solution)/shard_map/ppermute | solution.py:55
  35.6 2.8 %add_convert_fusion = bf16[64,3584]{1,0:T(8,128)(2,1)S(1)} fusion(bf16[64,3584]{1,0:T(8,128)(2,1)S(1)} %collective-permute-done, bf16[64,512]{1,0:T(8,128)(2,1)S(1)} %reshape.77, bf16[512,3584]{1,0:T(8,128)(2,1)} %bitcast.69), kind=kOutput, calls=%fused_computation.21 | convolution fusion | flops 235569152 | bytes 4653056 | tf_op jit(solution)/shard_map/dot_general | solution.py:103
  38.4 0.9 reshape.80
  39.3 4.0 %all-to-all-start.1 = ((bf16[16,4,3584]{2,1,0:T(4,128)(2,1)}), bf16[16,4,3584]{2,1,0:T(4,128)(2,1)S(1)}, u32[]{:S(2)}, u32[]{:S(2)}) async-start(bf16[16,4,3584]{2,1,0:T(4,128)(2,1)} %reshape.80), calls=%async_computation.1 | async-start | bytes 917504 | tf_op jit(solution)/shard_map/all_to_all | solution.py:111
  43.4 14.0 %all-to-all-done.1 = bf16[16,4,3584]{2,1,0:T(4,128)(2,1)S(1)} async-done(((bf16[16,4,3584]{2,1,0:T(4,128)(2,1)}), bf16[16,4,3584]{2,1,0:T(4,128)(2,1)S(1)}, u32[]{:S(2)}, u32[]{:S(2)}) %all-to-all-start.1) | async-done | bytes 458784 | tf_op jit(solution)/shard_map/all_to_all | solution.py:111
  57.4 0.2 convert_reduce_fusion
  57.8 0.3 convolution_convert_fusion.2
  58.1 0.2 copy.36
  58.3 11.9 %all_to_all.33 = bf16[16,2,3584]{2,1,0:T(2,128)(2,1)S(1)} all-to-all(bf16[16,2,3584]{2,1,0:T(2,128)(2,1)S(1)} %copy.36), channel_id=1, replica_groups=mesh['groups'=1,'ep'=16,'side'=2] {'ep'}, dimensions={0} | all-to-all | bytes 458752 | tf_op jit(solution)/shard_map/all_to_all | solution.py:134
  70.4 1.5 %collective-permute-done.1 = bf16[32,3584]{1,0:T(8,128)(2,1)S(1)} collective-permute-done((bf16[32,3584]{1,0:T(8,128)(2,1)S(1)}, bf16[32,3584]{1,0:T(8,128)(2,1)S(1)}, u32[]{:S(2)}, u32[]{:S(2)}) %collective-permute-start.1) | collective-permute-done | bytes 229408 | tf_op jit(solution)/shard_map/ppermute | solution.py:55
  71.9 2.8 %fusion.3 = f32[64,512]{1,0:T(8,128)S(1)} fusion(bf16[64,3584]{1,0:T(8,128)(2,1)S(1)} %constant_dynamic-update-slice_fusion, bf16[1,3584,512]{2,1,0:T(8,128)(2,1)} %param.24), kind=kOutput, calls=%fused_computation.7 | convolution fusion | flops 234881024 | bytes 4259840 | tf_op jit(solution)/shard_map/dot_general | solution.py:141
  74.7 4.6 %convolution_convert_fusion = bf16[64,3584]{1,0:T(8,128)(2,1)S(1)} fusion(bf16[1,512,3584]{2,1,0:T(8,128)(2,1)} %param.25, f32[64,512]{1,0:T(8,128)S(1)} %fusion.3, bf16[64,3584]{1,0:T(8,128)(2,1)S(1)} %constant_dynamic-update-slice_fusion, bf16[1,3584,512]{2,1,0:T(8,128)(2,1)} %param.23), kind=kOutput, calls=%fused_computation | convolution fusion | flops 470188032 | bytes 8388608 | tf_op jit(solution)/shard_map/dot_general | solution.py:143
  79.4 0.2 collective-permute-start.2
  79.6 1.4 %collective-permute-done.2 = bf16[32,3584]{1,0:T(8,128)(2,1)S(1)} collective-permute-done((bf16[32,3584]{1,0:T(8,128)(2,1)S(1)}, bf16[32,3584]{1,0:T(8,128)(2,1)S(1)}, u32[]{:S(2)}, u32[]{:S(2)}) %collective-permute-start.2) | collective-permute-done | bytes 229408 | tf_op jit(solution)/shard_map/ppermute | solution.py:55
  81.0 0.8 reshape.82
  81.7 3.7 %all-to-all-start.3 = ((bf16[16,2,3584]{2,1,0:T(2,128)(2,1)}), bf16[16,2,3584]{2,1,0:T(2,128)(2,1)S(1)}, u32[]{:S(2)}, u32[]{:S(2)}) async-start(bf16[16,2,3584]{2,1,0:T(2,128)(2,1)} %reshape.82), calls=%async_computation.3 | async-start | bytes 458752 | tf_op jit(solution)/shard_map/all_to_all | solution.py:150
  85.6 9.5 %all-to-all-done.3 = bf16[16,2,3584]{2,1,0:T(2,128)(2,1)S(1)} async-done(((bf16[16,2,3584]{2,1,0:T(2,128)(2,1)}), bf16[16,2,3584]{2,1,0:T(2,128)(2,1)S(1)}, u32[]{:S(2)}, u32[]{:S(2)}) %all-to-all-start.3) | async-done | bytes 229408 | tf_op jit(solution)/shard_map/all_to_all | solution.py:150
  95.0 0.9 fusion.1
  (34 shorter events, 1.2 us)
Async XLA Ops:
  0.0 1.1 %copy-start = (bf16[4,128,576]{1,2,0:T(8,128)(2,1)S(1)}, bf16[4,128,576]{1,2,0:T(8,128)(2,1)}, u32[]{:S(2)}) copy-start(bf16[4,128,576]{1,2,0:T(8,128)(2,1)} %param.13) | copy-start | bytes 1769476
  5.5 24.8 %copy-start.1 = (bf16[4,512,128]{2,1,0:T(8,128)(2,1)S(1)}, bf16[4,512,128]{2,1,0:T(8,128)(2,1)}, u32[]{:S(2)}) copy-start(bf16[4,512,128]{2,1,0:T(8,128)(2,1)} %param.19) | copy-start | bytes 1572868
  7.1 22.9 %all-to-all-start = ((bf16[4,128,512]{2,0,1:T(4,128)(2,1)}), bf16[4,128,512]{2,0,1:T(4,128)(2,1)S(1)}, u32[]{:S(2)}, u32[]{:S(2)}) async-start(bf16[4,128,512]{2,0,1:T(4,128)(2,1)} %copy.33), calls=%async_computation | async-start | bytes 1048576 | tf_op jit(solution)/shard_map/all_to_all | solution.py:91
  33.7 9.6 %copy-start.4 = (s32[4,8]{1,0:T(4,128)S(1)}, s32[4,8]{1,0:T(4,128)}, u32[]{:S(2)}) copy-start(s32[4,8]{1,0:T(4,128)} %param.21) | copy-start | bytes 388
  33.7 23.9 %copy-start.2 = (bf16[4,3584]{1,0:T(4,128)(2,1)S(1)}, bf16[4,3584]{1,0:T(4,128)(2,1)}, u32[]{:S(2)}) copy-start(bf16[4,3584]{1,0:T(4,128)(2,1)} %param.17) | copy-start | bytes 86020
  33.7 24.1 %copy-start.3 = (f32[3584]{0:T(1024)S(1)}, f32[3584]{0:T(1024)}, u32[]{:S(2)}) copy-start(f32[3584]{0:T(1024)} %param.18) | copy-start | bytes 43012
  33.7 1.9 %collective-permute-start = (bf16[64,3584]{1,0:T(8,128)(2,1)S(1)}, bf16[64,3584]{1,0:T(8,128)(2,1)S(1)}, u32[]{:S(2)}, u32[]{:S(2)}) collective-permute-start(bf16[64,3584]{1,0:T(8,128)(2,1)S(1)} %convolution_convert_fusion.1), channel_id=1, source_target_pairs={{0,1},{1,0},{2,3},{3,2},{4,5},{5,4},{6,7},{7,6},{8,9},{9,8},{10,11... | collective-permute-start | bytes 1376264 | tf_op jit(solution)/shard_map/ppermute | solution.py:55
  39.3 18.2 %all-to-all-start.1 = ((bf16[16,4,3584]{2,1,0:T(4,128)(2,1)}), bf16[16,4,3584]{2,1,0:T(4,128)(2,1)S(1)}, u32[]{:S(2)}, u32[]{:S(2)}) async-start(bf16[16,4,3584]{2,1,0:T(4,128)(2,1)} %reshape.80), calls=%async_computation.1 | async-start | bytes 917504 | tf_op jit(solution)/shard_map/all_to_all | solution.py:111
  70.3 1.6 %collective-permute-start.1 = (bf16[32,3584]{1,0:T(8,128)(2,1)S(1)}, bf16[32,3584]{1,0:T(8,128)(2,1)S(1)}, u32[]{:S(2)}, u32[]{:S(2)}) collective-permute-start(bf16[32,3584]{1,0:T(8,128)(2,1)S(1)} %reshape.81), channel_id=1, source_target_pairs={{0,1},{1,0},{2,3},{3,2},{4,5},{5,4},{6,7},{7,6},{8,9},{9,8},{10,11... | collective-permute-start | bytes 688136 | tf_op jit(solution)/shard_map/ppermute | solution.py:55
  74.7 10.8 %copy-start.5 = (f32[4,8]{1,0:T(4,128)S(1)}, f32[4,8]{1,0:T(4,128)}, u32[]{:S(2)}) copy-start(f32[4,8]{1,0:T(4,128)} %param.22) | copy-start | bytes 388
  79.4 1.6 %collective-permute-start.2 = (bf16[32,3584]{1,0:T(8,128)(2,1)S(1)}, bf16[32,3584]{1,0:T(8,128)(2,1)S(1)}, u32[]{:S(2)}, u32[]{:S(2)}) collective-permute-start(bf16[32,3584]{1,0:T(8,128)(2,1)S(1)} %slice.20), channel_id=1, source_target_pairs={{0,1},{1,0},{2,3},{3,2},{4,5},{5,4},{6,7},{7,6},{8,9},{9,8},{10,11... | collective-permute-start | bytes 688136 | tf_op jit(solution)/shard_map/ppermute | solution.py:55
  81.7 13.3 %all-to-all-start.3 = ((bf16[16,2,3584]{2,1,0:T(2,128)(2,1)}), bf16[16,2,3584]{2,1,0:T(2,128)(2,1)S(1)}, u32[]{:S(2)}, u32[]{:S(2)}) async-start(bf16[16,2,3584]{2,1,0:T(2,128)(2,1)} %reshape.82), calls=%async_computation.3 | async-start | bytes 458752 | tf_op jit(solution)/shard_map/all_to_all | solution.py:150

commit v2 on v0

v2 whole, which is shorter than its diff:
```python
import functools

import jax
import jax.numpy as jnp
from jax import lax
from jax.experimental import pallas as pl
from jax.experimental.pallas import tpu as pltpu
from jax.sharding import PartitionSpec as P

LAT = 512
QKD = 192
LANES = 128


norm_epsilon = 1e-06
masked_score = -1e30

VMEM_SPEC = pl.BlockSpec(memory_space=pltpu.VMEM)
HBM_SPEC = pl.BlockSpec(memory_space=pltpu.HBM)


def stay(array):
    return pltpu.with_memory_space_constraint(array, pltpu.HBM)


def place(array):
    return pltpu.with_memory_space_constraint(array, pltpu.VMEM)


def attention_kernel(
    lengths_hbm,
    queries_hbm,
    cache_hbm,
    fresh_hbm,
    up_hbm,
    project_hbm,
    out_ref,
    up_ref,
    project_ref,
    lengths_ref,
    queries_ref,
    cache_ref,
    fresh_ref,
    rows_ref,
    placed_ref,
    sems,
):
    requests = cache_hbm.shape[0]
    positions = queries_hbm.shape[0] // requests
    first = [
        pltpu.make_async_copy(lengths_hbm, lengths_ref, sems.at[0]),
        pltpu.make_async_copy(fresh_hbm, fresh_ref, sems.at[1]),
    ]
    pieces = []
    for r in range(requests):
        tokens_of = pl.ds(r * positions, positions)
        pieces.append(
            [
                pltpu.make_async_copy(cache_hbm.at[r], cache_ref.at[r], sems.at[2 + 2 * r]),
                pltpu.make_async_copy(
                    queries_hbm.at[tokens_of], queries_ref.at[tokens_of], sems.at[3 + 2 * r]
                ),
            ]
        )
    count = 2 + 2 * requests
    loads = [
        pltpu.make_async_copy(up_hbm, up_ref, sems.at[count]),
        pltpu.make_async_copy(project_hbm, project_ref, sems.at[count + 1]),
    ]
    for copy in first + sum(pieces, []) + loads:
        copy.start()
    for copy in first:
        copy.wait()
    factor = 1.0 / QKD**0.5
    tokens, _, heads = queries_ref.shape
    holders, block, latent_width = out_ref.shape
    own_heads = block // tokens
    fresh_rows = -(-positions // 8) * 8
    for r in range(requests):
        for copy in pieces[r]:
            copy.wait()
        keys = jnp.transpose(cache_ref[r])
        wanted = jnp.concatenate(
            [queries_ref[r * positions + j] for j in range(positions)], axis=1
        )
        fresh = fresh_ref[r * positions : (r + 1) * positions, :]
        cache_scores = jnp.dot(keys, wanted, preferred_element_type=jnp.float32) * factor
        padded = jnp.concatenate(
            [fresh, jnp.zeros((16 - positions, fresh.shape[1]), fresh.dtype)], axis=0
        )
        fresh_scores = (
            jnp.dot(padded, wanted, preferred_element_type=jnp.float32)[:fresh_rows] * factor
        )
        cache_live = lax.broadcasted_iota(jnp.int32, cache_scores.shape, 0) < lengths_ref[r]
        fresh_row = lax.broadcasted_iota(jnp.int32, fresh_scores.shape, 0)
        step = lax.broadcasted_iota(jnp.int32, fresh_scores.shape, 1) // heads
        fresh_live = fresh_row <= step
        cache_scores = jnp.where(cache_live, cache_scores, masked_score)
        fresh_scores = jnp.where(fresh_live, fresh_scores, masked_score)
        highest = jnp.maximum(
            jnp.max(cache_scores, axis=0, keepdims=True),
            jnp.max(fresh_scores, axis=0, keepdims=True),
        )
        cache_weight = jnp.where(cache_live, jnp.exp(cache_scores - highest), 0.0)
        fresh_weight = jnp.where(fresh_live, jnp.exp(fresh_scores - highest), 0.0)
        total = jnp.sum(cache_weight, axis=0, keepdims=True) + jnp.sum(
            fresh_weight, axis=0, keepdims=True
        )
        side_columns = jnp.where(fresh_row == positions, total, fresh_weight)
        for j in range(positions):
            lanes = slice(j * heads, (j + 1) * heads)
            columns = jnp.transpose(side_columns[:, lanes])
            weights = jnp.transpose(cache_weight[:, lanes]).astype(jnp.bfloat16)
            merged = jnp.dot(
                weights, keys[:, :latent_width], preferred_element_type=jnp.float32
            )
            for q in range(j + 1):
                merged = merged + columns[:, q : q + 1].astype(jnp.bfloat16).astype(
                    jnp.float32
                ) * fresh[q : q + 1, :latent_width].astype(jnp.float32)
            merged = merged / columns[:, positions : positions + 1]
            token = r * positions + j
            for part in range(latent_width // LANES):
                rows_ref[part] = merged[:, part * LANES : (part + 1) * LANES]
                for i in range(own_heads):
                    placed_ref[part, pl.ds(token * own_heads + i, holders, stride=block), :] = (
                        rows_ref[part, pl.ds(i, holders, stride=own_heads), :]
                    )
    for part in range(latent_width // LANES):
        out_ref[:, :, part * LANES : (part + 1) * LANES] = (
            placed_ref[part].astype(jnp.bfloat16).reshape(holders, block, LANES)
        )
    for copy in loads:
        copy.wait()


def attend(queries, latent_cache, new_latent, lengths, value_up, flat_out, holders):
    tokens, heads, _ = queries.shape
    requests = latent_cache.shape[0]
    block = tokens * heads // holders
    operands = (lengths, jnp.swapaxes(queries, 1, 2), jnp.swapaxes(latent_cache, 1, 2), new_latent)
    return pl.pallas_call(
        attention_kernel,
        out_shape=[
            jax.ShapeDtypeStruct((holders, block, LAT), jnp.bfloat16),
            pltpu.VMEM(value_up.shape, value_up.dtype),
            pltpu.VMEM(flat_out.shape, flat_out.dtype),
        ],
        in_specs=[HBM_SPEC] * 6,
        out_specs=[VMEM_SPEC] * 3,
        scratch_shapes=[pltpu.SMEM(lengths.shape, lengths.dtype)]
        + [pltpu.VMEM(x.shape, x.dtype) for x in operands[1:]]
        + [
            pltpu.VMEM((LAT // LANES, heads, LANES), jnp.float32),
            pltpu.VMEM((LAT // LANES, tokens * heads, LANES), jnp.float32),
            pltpu.SemaphoreType.DMA((4 + 2 * requests,)),
        ],
        compiler_params=pltpu.CompilerParams(vmem_limit_bytes=16 << 20),
    )(*map(stay, operands + (value_up, flat_out)))


def column_step(width):
    for step in (512, 384, 256, 128):
        if width % step == 0:
            return step
    return width


def head_kernel(
    arrived_ref, up_ref, out_ref, gate_hbm, send_ref, own_ref, gate_ref, wide_ref, sem
):
    load = pltpu.make_async_copy(gate_hbm, gate_ref, sem)
    load.start()
    tokens_in = arrived_ref.shape[1] // up_ref.shape[0]
    sources, block, latent_width = arrived_ref.shape
    own_heads, _, value_width = up_ref.shape
    step = column_step(out_ref.shape[1])
    steps = out_ref.shape[1] // step
    rows = sources * tokens_in
    parts = latent_width // LANES
    for part in range(parts):
        wide_ref[part] = (
            arrived_ref[:, :, part * LANES : (part + 1) * LANES]
            .reshape(sources * block, LANES)
            .astype(jnp.float32)
        )
    outs = []
    for i in range(own_heads):
        latent = jnp.concatenate(
            [
                wide_ref[part, pl.ds(i, rows, stride=own_heads), :].astype(jnp.bfloat16)
                for part in range(parts)
            ],
            axis=1,
        )
        outs.append(
            jnp.dot(latent, up_ref[i], preferred_element_type=jnp.float32).astype(jnp.bfloat16)
        )
    heads = jnp.concatenate(outs, axis=1)
    side = lax.axis_index("side")
    half = rows // 2
    target = lax.broadcasted_iota(jnp.int32, (rows, rows), 0)
    source = lax.broadcasted_iota(jnp.int32, (rows, rows), 1)
    within = jnp.where(target < half, target, target - half)
    wanted_side = jnp.where(target < half, side, 1 - side)
    origin = (within // tokens_in) * (2 * tokens_in) + wanted_side * tokens_in + within % tokens_in
    sorter = jnp.where(source == origin, 1.0, 0.0).astype(jnp.bfloat16)
    ordered = jnp.dot(sorter, heads, preferred_element_type=jnp.float32).astype(jnp.bfloat16)
    own_ref[...] = ordered[:half]
    other = ordered[half:]
    for k in range(steps):
        columns = slice(k * step, (k + 1) * step)
        send_ref[:, columns] = jnp.dot(
            other, out_ref[:, columns], preferred_element_type=jnp.float32
        ).astype(jnp.bfloat16)
    load.wait()


def project_heads(arrived, value_up, flat_out, gate):
    sources, block, _ = arrived.shape
    own_heads, latent_width, value_width = value_up.shape
    half = sources * block // own_heads // 2
    feature = flat_out.shape[1]
    return pl.pallas_call(
        head_kernel,
        out_shape=[
            jax.ShapeDtypeStruct((half, feature), jnp.bfloat16),
            jax.ShapeDtypeStruct((half, own_heads * value_width), jnp.bfloat16),
            pltpu.VMEM(gate.shape, gate.dtype),
        ],
        in_specs=[VMEM_SPEC] * 3 + [HBM_SPEC],
        out_specs=[VMEM_SPEC] * 3,
        scratch_shapes=[
            pltpu.VMEM((latent_width // LANES, sources * block, LANES), jnp.float32),
            pltpu.SemaphoreType.DMA,
        ],
        compiler_params=pltpu.CompilerParams(vmem_limit_bytes=16 << 20),
    )(place(arrived), place(value_up), place(flat_out), stay(gate))


def own_kernel(heads_ref, out_ref, up_hbm, keep_ref, up_ref, sem):
    load = pltpu.make_async_copy(up_hbm, up_ref, sem)
    load.start()
    step = column_step(out_ref.shape[1])
    for k in range(out_ref.shape[1] // step):
        columns = slice(k * step, (k + 1) * step)
        keep_ref[:, columns] = jnp.dot(
            heads_ref[...], out_ref[:, columns], preferred_element_type=jnp.float32
        )
    load.wait()


def project_own(heads, flat_out, up):
    rows, feature = heads.shape[0], flat_out.shape[1]
    return pl.pallas_call(
        own_kernel,
        out_shape=[
            jax.ShapeDtypeStruct((rows, feature), jnp.float32),
            pltpu.VMEM(up.shape, up.dtype),
        ],
        in_specs=[VMEM_SPEC] * 2 + [HBM_SPEC],
        out_specs=[VMEM_SPEC] * 2,
        scratch_shapes=[pltpu.SemaphoreType.DMA],
        compiler_params=pltpu.CompilerParams(vmem_limit_bytes=4 << 20),
        cost_estimate=pl.CostEstimate(
            flops=2 * rows * flat_out.size,
            bytes_accessed=2 * flat_out.size + 2 * up.size,
            transcendentals=0,
        ),
    )(place(heads), place(flat_out), stay(up))


def sum_kernel(keep_ref, other_ref, out_ref):
    groups, rows, feature = out_ref.shape
    step = column_step(feature)
    for k in range(feature // step):
        columns = slice(k * step, (k + 1) * step)
        total = keep_ref[:, columns].astype(jnp.float32) + other_ref[:, columns].astype(
            jnp.float32
        )
        out_ref[:, :, columns] = total.astype(jnp.bfloat16).reshape(groups, rows, step)


def sum_halves(keep, other, groups):
    count, feature = keep.shape
    return pl.pallas_call(
        sum_kernel,
        out_shape=jax.ShapeDtypeStruct((groups, count // groups, feature), jnp.bfloat16),
        in_specs=[VMEM_SPEC] * 2,
        out_specs=VMEM_SPEC,
        compiler_params=pltpu.CompilerParams(vmem_limit_bytes=4 << 20),
    )(place(keep), place(other))


def stream_kernel(
    shared_ref,
    residual_ref,
    gain_ref,
    ids_ref,
    share_ref,
    rows_ref,
    stream_ref,
    coefficient_ref,
):
    tokens, feature = residual_ref.shape
    experts, capacity, _ = rows_ref.shape
    slots = coefficient_ref.shape[1]
    step = column_step(feature)
    blocks = [slice(k * step, (k + 1) * step) for k in range(feature // step)]
    square = jnp.zeros((tokens, 1), jnp.float32)
    for columns in blocks:
        attention = jnp.sum(shared_ref[:, :, columns].astype(jnp.float32), axis=0)
        stream = residual_ref[:, columns].astype(jnp.float32) + attention
        stream_ref[:, columns] = stream
        square = square + jnp.sum(stream * stream, axis=1, keepdims=True)
    scale = lax.rsqrt(square / feature + norm_epsilon)

    slot = lax.broadcasted_iota(jnp.int32, (tokens, slots), 1)
    expert = slot // capacity
    row = lax.broadcasted_iota(jnp.int32, (tokens, slots), 0)
    picked = jnp.zeros((tokens, slots), jnp.int32)
    share = jnp.zeros((tokens, slots), jnp.float32)
    for k in range(ids_ref.shape[1]):
        same = ids_ref[:, k : k + 1] == expert
        picked = picked + jnp.where(same, 1, 0)
        share = share + jnp.where(same, share_ref[:, k : k + 1], 0.0)
    before = jnp.zeros((tokens, slots), jnp.int32)
    for t in range(tokens - 1):
        before = before + jnp.where(row > t, picked[t : t + 1, :], 0)
    placed = (picked > 0) & (before == slot % capacity)
    coefficient_ref[...] = jnp.where(placed, share, 0.0)
    padded = jnp.concatenate(
        [jnp.where(placed, 1.0, 0.0), jnp.zeros((8 - tokens, slots), jnp.float32)], axis=0
    )
    chooser = jnp.transpose(padded)[: experts * capacity].astype(jnp.bfloat16)
    for columns in blocks:
        gain = jnp.concatenate(
            [
                gain_ref[part : part + 1, :]
                for part in range(columns.start // LANES, columns.stop // LANES)
            ],
            axis=1,
        )
        normed = stream_ref[:, columns] * scale * gain
        normed = jnp.concatenate(
            [normed, jnp.zeros((8 - tokens, step), jnp.float32)], axis=0
        ).astype(jnp.bfloat16)
        chosen = jnp.dot(chooser, normed, preferred_element_type=jnp.float32)
        rows_ref[:, :, columns] = chosen.astype(jnp.bfloat16).reshape(experts, capacity, step)


def route(shared, residual, gain, expert_ids, expert_weights, capacity):
    experts, tokens, feature = shared.shape
    slots = -(-experts * capacity // LANES) * LANES
    return pl.pallas_call(
        stream_kernel,
        out_shape=[
            jax.ShapeDtypeStruct((experts, capacity, feature), jnp.bfloat16),
            jax.ShapeDtypeStruct((tokens, feature), jnp.float32),
            jax.ShapeDtypeStruct((tokens, slots), jnp.float32),
        ],
        in_specs=[VMEM_SPEC] * 5,
        out_specs=[VMEM_SPEC] * 3,
        compiler_params=pltpu.CompilerParams(vmem_limit_bytes=4 << 20),
    )(place(shared), residual, gain.reshape(feature // LANES, LANES), expert_ids, expert_weights)


def mix_kernel(returned_ref, coefficient_ref, stream_ref, out_ref):
    experts, capacity, feature = returned_ref.shape
    tokens = stream_ref.shape[0]
    count = experts * capacity
    rest = coefficient_ref[:, :count]
    terms = []
    for _ in range(3):
        term = rest.astype(jnp.bfloat16).astype(jnp.float32)
        rest = rest - term
        terms.append(term)
    terms.append(jnp.zeros_like(rest))
    weights = jnp.concatenate(terms, axis=0).astype(jnp.bfloat16)
    step = column_step(feature)
    for k in range(feature // step):
        columns = slice(k * step, (k + 1) * step)
        parts = jnp.dot(
            weights,
            returned_ref[:, :, columns].reshape(count, step),
            preferred_element_type=jnp.float32,
        )
        mixture = parts[:tokens] + parts[tokens : 2 * tokens] + parts[2 * tokens : 3 * tokens]
        out_ref[:, columns] = (stream_ref[:, columns] + mixture).astype(jnp.bfloat16)


def mix(returned, coefficient, stream):
    return pl.pallas_call(
        mix_kernel,
        out_shape=jax.ShapeDtypeStruct(stream.shape, jnp.bfloat16),
        in_specs=[VMEM_SPEC] * 3,
        out_specs=VMEM_SPEC,
        compiler_params=pltpu.CompilerParams(vmem_limit_bytes=4 << 20),
    )(place(returned), place(coefficient), place(stream))


def expert_kernel(
    own_rows_ref,
    other_rows_ref,
    gate_ref,
    up_ref,
    down_hbm,
    keep_ref,
    send_ref,
    down_ref,
    hidden_ref,
    sem,
):
    load = pltpu.make_async_copy(down_hbm, down_ref, sem)
    load.start()
    width = gate_ref.shape[1]
    feature = down_hbm.shape[1]
    hidden_step = 256 if width % 256 == 0 else width
    step = column_step(feature)
    shape = own_rows_ref.shape
    own_count = shape[0] * shape[1]
    rows = jnp.concatenate(
        [
            own_rows_ref[...].reshape(own_count, shape[2]),
            other_rows_ref[...].reshape(own_count, shape[2]),
        ]
    )
    for k in range(width // hidden_step):
        columns = slice(k * hidden_step, (k + 1) * hidden_step)
        gate_part = jnp.dot(rows, gate_ref[:, columns], preferred_element_type=jnp.float32)
        up_part = jnp.dot(rows, up_ref[:, columns], preferred_element_type=jnp.float32)
        hidden_ref[:, columns] = (gate_part / (1.0 + jnp.exp(-gate_part)) * up_part).astype(
            jnp.bfloat16
        )
    hidden = hidden_ref[...]
    load.wait()
    for k in range(feature // step):
        columns = slice(k * step, (k + 1) * step)
        out = jnp.dot(hidden, down_ref[:, columns], preferred_element_type=jnp.float32).astype(
            jnp.bfloat16
        )
        keep_ref[:, columns] = out[:own_count]
        send_ref[:, columns] = out[own_count:]


def expert_halves(own_rows, other_rows, gate, up, down):
    count, feature = own_rows.shape[0] * own_rows.shape[1], own_rows.shape[2]
    return pl.pallas_call(
        expert_kernel,
        out_shape=[jax.ShapeDtypeStruct((count, feature), jnp.bfloat16)] * 2,
        in_specs=[VMEM_SPEC] * 4 + [HBM_SPEC],
        out_specs=[VMEM_SPEC] * 2,
        scratch_shapes=[
            pltpu.VMEM(down.shape, down.dtype),
            pltpu.VMEM((2 * count, gate.shape[1]), jnp.bfloat16),
            pltpu.SemaphoreType.DMA,
        ],
        compiler_params=pltpu.CompilerParams(vmem_limit_bytes=16 << 20),
    )(place(own_rows), place(other_rows), place(gate), place(up), stay(down))


def swap_sides(block):
    return lax.ppermute(block, "side", [(0, 1), (1, 0)])


def local(
    queries,
    latent_cache,
    new_latent,
    lengths,
    residual,
    norm_gain,
    value_up,
    output_proj,
    expert_ids,
    expert_weights,
    gate_proj,
    up_proj,
    down_proj,
):
    row_count = queries.shape[0]
    feature = residual.shape[1]
    ep_count = lax.axis_size("ep")
    side_count = lax.axis_size("side")
    assert side_count == 2
    flat_out = output_proj.reshape(output_proj.shape[0] * output_proj.shape[1], feature)
    capacity = min(
        row_count, max(2, (row_count * expert_ids.shape[1] + ep_count - 1) // ep_count)
    )

    latent, value_up, flat_out = attend(
        queries, latent_cache, new_latent, lengths, value_up, flat_out, ep_count * side_count
    )
    arrived = lax.all_to_all(latent, ("ep", "side"), split_axis=0, concat_axis=0, tiled=True)
    send, own_heads, gate = project_heads(arrived, value_up, flat_out, gate_proj[0])
    from_other = swap_sides(send)
    keep, up = project_own(own_heads, flat_out, up_proj[0])
    contribution = sum_halves(keep, from_other, ep_count)
    shared = lax.all_to_all(contribution, "ep", split_axis=0, concat_axis=0, tiled=True)
    outbound, stream, coefficient = route(
        shared, residual, norm_gain, expert_ids, expert_weights, capacity
    )
    own_rows = lax.all_to_all(outbound, "ep", split_axis=0, concat_axis=0, tiled=True)
    other_rows = swap_sides(own_rows)
    keep, send = expert_halves(own_rows, other_rows, gate, up, down_proj[0])
    both = sum_halves(keep, swap_sides(send), ep_count)
    returned = lax.all_to_all(both, "ep", split_axis=0, concat_axis=0, tiled=True)
    return mix(returned, coefficient, stream)


def solution(mesh):
    in_specs = (
        P(("groups", "ep", "side"), None, None),
        P(("groups", "ep", "side"), None, None),
        P(("groups", "ep", "side"), None),
        P(("groups", "ep", "side")),
        P(("groups", "ep", "side"), None),
        P(),
        P(("ep", "side"), None, None),
        P(("ep", "side"), None, None),
        P(("groups", "ep", "side"), None),
        P(("groups", "ep", "side"), None),
        P("ep", None, "side"),
        P("ep", None, "side"),
        P("ep", "side", None),
    )
    out_specs = P(("groups", "ep", "side"), None)
    return jax.shard_map(local, mesh=mesh, in_specs=in_specs, out_specs=out_specs, check_vma=False)
```

time: 216 us -> 82.1 us (0.38)
  waiting for transfers between devices: 135 us -> 2.84 us
  blocking collectives: 41 us -> 66.1 us
  matrix products: 17.9 us -> 0 us
  between operations: 14 us -> 0.11 us
  Pallas kernels: 0 us -> 12.5 us
  local copies, waits for them, and re-layouts: 2.8 us -> 0.03 us
  starting transfers between devices: 2.87 us -> 0.27 us
    unnamed x4 -> x0, waiting for transfers between devices: 113 us -> none
    all_to_all x2 -> x4, blocking collectives: 41 us -> 66.1 us  [the longest x1 22.7 us: local(): lax.all_to_all(latent, ('ep', 'side'), split_axis=0, concat_axis=0, tiled...]
    dot_general x9 -> x0, matrix products: 17.9 us -> none  [the longest x1 6.09 us: local(): jnp.dot(head_flat, flat_out, preferred_element_type=jnp.float32)]
    all_to_all x1 -> x0, waiting for transfers between devices: 14.3 us -> none  [local(): lax.all_to_all(partial_out, ('ep', 'side'), split_axis=0, concat_axis=0,...]
    pallas_call x0 -> x8, Pallas kernels: none -> 12.5 us  [the longest x1 4.02 us: expert_halves(): pl.pallas_call(expert_kernel, out_shape=[jax.ShapeDtypeStruct((count, fea...]
    all_gather x2 -> x0, waiting for transfers between devices: 8.31 us -> none  [the longest x1 8.29 us: local(): lax.all_gather(output_proj, 'side', axis=0, tiled=True)]
    ppermute x0 -> x3, waiting for transfers between devices: none -> 2.84 us  [swap_sides(): return lax.ppermute(block, 'side', [(0, 1), (1, 0)])]
    all_to_all x1 -> x0, starting transfers between devices: 2.76 us -> none  [local(): lax.all_to_all(partial_out, ('ep', 'side'), split_axis=0, concat_axis=0,...]
  transfers between devices with their start and end apart: 4 -> 3, of which waited for: 3 -> 2; matrix products, arithmetic and copies ran while one was open for 1% -> 0% of each run, Pallas kernels for 0% -> 3%
where the time goes in v2:
time: 82.1 us; the launch traced here: 81.8 us
  blocking collectives  66.1 us (81%)
  Pallas kernels  12.5 us (15%)
  waiting for transfers between devices  2.84 us (3%)
    all_to_all x1, blocking collectives, local(): lax.all_to_all(latent, ('ep', 'side'), split_axis=0, concat_axis=0, tiled...  22.7 us
    all_to_all x1, blocking collectives, local(): lax.all_to_all(contribution, 'ep', split_axis=0, concat_axis=0, tiled=True)  18.1 us
    all_to_all x1, blocking collectives, local(): lax.all_to_all(both, 'ep', split_axis=0, concat_axis=0, tiled=True)  13.1 us
    all_to_all x1, blocking collectives, local(): lax.all_to_all(outbound, 'ep', split_axis=0, concat_axis=0, tiled=True)  12.1 us
    pallas_call x1, Pallas kernels, expert_halves(): pl.pallas_call(expert_kernel, out_shape=[jax.ShapeDtypeStruct((count, fea...  4.02 us
    pallas_call x1, Pallas kernels, attend(): pl.pallas_call(attention_kernel, out_shape=[jax.ShapeDtypeStruct((holders...  2.91 us
    ppermute x3, waiting for transfers between devices, swap_sides(): return lax.ppermute(block, 'side', [(0, 1), (1, 0)])  2.84 us
    pallas_call x1, Pallas kernels, project_own(): pl.pallas_call(own_kernel, out_shape=[jax.ShapeDtypeStruct((rows, feature...  2.07 us
  transfers between devices with their start and end apart: 3, of which 2 were waited for; matrix products, arithmetic and copies ran while one was open for 0% of the time, Pallas kernels for 3%

profile of v2, /device:TPU:0, one launch (start us, length us, event | category | flops | bytes accessed | tf_op | source)
XLA Modules:
  0.0 81.8 jit_solution(12170074445516663377)
XLA Ops:
  0.0 2.9 %shard_map.127 = (bf16[32,16,512]{2,1,0:T(8,128)(2,1)S(1)}, bf16[4,512,128]{2,1,0:T(8,128)(2,1)S(1)}, bf16[512,3584]{1,0:T(8,128)(2,1)S(1)}) custom-call(s32[2]{0:T(128)} %lengths_hbm.1, bf16[4,576,128]{2,1,0:T(8,128)(2,1)} %bitcast.12, bf16[2,576,128]{2,1,0:T(8,128)(2,1)} %bitcast.13, bf16[4,576]{1,0:T(4,128)(2,1)} %fresh_hbm.1, ...), custom_call_target="tpu_custom_call" | custom-call | tf_op jit(solution)/shard_map/pallas_call | solution.py:142
  2.9 22.7 %all_to_all.20.arrived_ref = bf16[32,16,512]{2,1,0:T(8,128)(2,1)S(1)} all-to-all(bf16[32,16,512]{2,1,0:T(8,128)(2,1)S(1)} %get-tuple-element.18), channel_id=1, replica_groups=mesh['groups'=1,'ep'=16,'side'=2] {'ep','side'}, dimensions={0} | all-to-all | bytes 1048576 | tf_op jit(solution)/shard_map/all_to_all | solution.py:494
  25.7 2.0 %shard_map.128 = (bf16[64,3584]{1,0:T(8,128)(2,1)S(1)}, bf16[64,512]{1,0:T(8,128)(2,1)S(1)}, bf16[3584,512]{1,0:T(8,128)(2,1)S(1)}) custom-call(bf16[32,16,512]{2,1,0:T(8,128)(2,1)S(1)} %all_to_all.20.arrived_ref, bf16[4,512,128]{2,1,0:T(8,128)(2,1)S(1)} %get-tuple-element.19.up_ref, bf16[512,3584]{1,0:T(8,128)(2,1)S(1)} %get-tuple-element.20.out_ref, ...), custom_call_target="tpu_custom_call" | custom-call | tf_op jit(solution)/shard_map/pallas_call | solution.py:224
  27.7 0.1 collective-permute-start
  27.8 0.0 copy-start
  27.8 0.0 copy-start.1
  27.8 0.0 copy-start.2
  27.8 0.0 copy-start.3
  27.8 2.1 %shard_map.129 = (f32[64,3584]{1,0:T(8,128)S(1)}, bf16[3584,512]{1,0:T(8,128)(2,1)S(1)}) custom-call(bf16[64,512]{1,0:T(8,128)(2,1)S(1)} %get-tuple-element.21.heads_ref, bf16[512,3584]{1,0:T(8,128)(2,1)S(1)} %get-tuple-element.20.out_ref, bf16[3584,512]{1,0:T(8,128)(2,1)} %bitcast.9), custom_call_target="tpu_custom_call" | custom-call | flops 234881024 | bytes 7340032 | tf_op jit(solution)/shard_map/pallas_call | solution.py:255
  29.9 0.0 collective-permute-done.other_ref
  29.9 0.1 shard_map.130
  30.1 18.1 %all_to_all.21.shared_ref = bf16[16,4,3584]{2,1,0:T(4,128)(2,1)S(1)} all-to-all(bf16[16,4,3584]{2,1,0:T(4,128)(2,1)S(1)} %shard_map.130), channel_id=1, replica_groups=mesh['groups'=1,'ep'=16,'side'=2] {'ep'}, dimensions={0} | all-to-all | bytes 917504 | tf_op jit(solution)/shard_map/all_to_all | solution.py:499
  48.2 0.0 copy-done
  48.2 0.0 copy-done.1
  48.2 0.0 copy-done.2
  48.2 0.0 copy-done.3
  48.2 0.5 shard_map.131
  48.7 12.1 %all_to_all.22.own_rows_ref = bf16[16,2,3584]{2,1,0:T(2,128)(2,1)S(1)} all-to-all(bf16[16,2,3584]{2,1,0:T(2,128)(2,1)S(1)} %get-tuple-element.24), channel_id=1, replica_groups=mesh['groups'=1,'ep'=16,'side'=2] {'ep'}, dimensions={0} | all-to-all | bytes 458752 | tf_op jit(solution)/shard_map/all_to_all | solution.py:503
  60.8 0.0 collective-permute-start.1
  60.8 1.5 %collective-permute-done.1.other_rows_ref = bf16[16,2,3584]{2,1,0:T(2,128)(2,1)S(1)} collective-permute-done((bf16[16,2,3584]{2,1,0:T(2,128)(2,1)S(1)}, bf16[16,2,3584]{2,1,0:T(2,128)(2,1)S(1)}, u32[]{:S(2)}, u32[]{:S(2)}) %collective-permute-start.1) | collective-permute-done | bytes 229408 | tf_op jit(solution)/shard_map/ppermute | solution.py:463
  62.3 4.0 %shard_map.132 = (bf16[32,3584]{1,0:T(8,128)(2,1)S(1)}, bf16[32,3584]{1,0:T(8,128)(2,1)S(1)}) custom-call(bf16[16,2,3584]{2,1,0:T(2,128)(2,1)S(1)} %all_to_all.22.own_rows_ref, bf16[16,2,3584]{2,1,0:T(2,128)(2,1)S(1)} %collective-permute-done.1.other_rows_ref, bf16[3584,512]{1,0:T(8,128)(2,1)S(1)} %get-tuple-element.25.gate_ref, ...), custom_call_target="tpu_custom_call" | custom-call | tf_op jit(solution)/shard_map/pallas_call | solution.py:448
  66.3 0.2 collective-permute-start.2
  66.5 1.4 %collective-permute-done.2.other_ref = bf16[32,3584]{1,0:T(8,128)(2,1)S(1)} collective-permute-done((bf16[32,3584]{1,0:T(8,128)(2,1)S(1)}, bf16[32,3584]{1,0:T(8,128)(2,1)S(1)}, u32[]{:S(2)}, u32[]{:S(2)}) %collective-permute-start.2) | collective-permute-done | bytes 229408 | tf_op jit(solution)/shard_map/ppermute | solution.py:463
  67.9 0.1 shard_map.133
  67.9 13.1 %all_to_all.23.returned_ref = bf16[16,2,3584]{2,1,0:T(2,128)(2,1)S(1)} all-to-all(bf16[16,2,3584]{2,1,0:T(2,128)(2,1)S(1)} %shard_map.133), channel_id=1, replica_groups=mesh['groups'=1,'ep'=16,'side'=2] {'ep'}, dimensions={0} | all-to-all | bytes 458752 | tf_op jit(solution)/shard_map/all_to_all | solution.py:507
  81.0 0.8 shard_map.134
Async XLA Ops:
  27.7 2.2 %collective-permute-start = (bf16[64,3584]{1,0:T(8,128)(2,1)S(1)}, bf16[64,3584]{1,0:T(8,128)(2,1)S(1)}, u32[]{:S(2)}, u32[]{:S(2)}) collective-permute-start(bf16[64,3584]{1,0:T(8,128)(2,1)S(1)} %get-tuple-element.23), channel_id=1, source_target_pairs={{0,1},{1,0},{2,3},{3,2},{4,5},{5,4},{6,7},{7,6},{8,9},{9,8},{10,11... | collective-permute-start | bytes 1376264 | tf_op jit(solution)/shard_map/ppermute | solution.py:463
  27.8 20.4 %copy-start = (bf16[4,3584]{1,0:T(4,128)(2,1)S(1)}, bf16[4,3584]{1,0:T(4,128)(2,1)}, u32[]{:S(2)}) copy-start(bf16[4,3584]{1,0:T(4,128)(2,1)} %residual_ref.1) | copy-start | bytes 86020
  27.8 20.4 %copy-start.1 = (f32[3584]{0:T(1024)S(1)}, f32[3584]{0:T(1024)}, u32[]{:S(2)}) copy-start(f32[3584]{0:T(1024)} %param.18) | copy-start | bytes 43012
  27.8 20.4 %copy-start.2 = (s32[4,8]{1,0:T(4,128)S(1)}, s32[4,8]{1,0:T(4,128)}, u32[]{:S(2)}) copy-start(s32[4,8]{1,0:T(4,128)} %ids_ref.1) | copy-start | bytes 388
  27.8 20.4 %copy-start.3 = (f32[4,8]{1,0:T(4,128)S(1)}, f32[4,8]{1,0:T(4,128)}, u32[]{:S(2)}) copy-start(f32[4,8]{1,0:T(4,128)} %share_ref.1) | copy-start | bytes 388
  60.8 1.5 %collective-permute-start.1 = (bf16[16,2,3584]{2,1,0:T(2,128)(2,1)S(1)}, bf16[16,2,3584]{2,1,0:T(2,128)(2,1)S(1)}, u32[]{:S(2)}, u32[]{:S(2)}) collective-permute-start(bf16[16,2,3584]{2,1,0:T(2,128)(2,1)S(1)} %all_to_all.22.own_rows_ref), channel_id=1, source_target_pairs={{0,1},{1,0},{2,3},{3,2},{4,5},{5,4},{6,7},{7,6},{8,9},{9,8},{10,11... | collective-permute-start | bytes 688136 | tf_op jit(solution)/shard_map/ppermute | solution.py:463
  66.3 1.6 %collective-permute-start.2 = (bf16[32,3584]{1,0:T(8,128)(2,1)S(1)}, bf16[32,3584]{1,0:T(8,128)(2,1)S(1)}, u32[]{:S(2)}, u32[]{:S(2)}) collective-permute-start(bf16[32,3584]{1,0:T(8,128)(2,1)S(1)} %get-tuple-element.28), channel_id=1, source_target_pairs={{0,1},{1,0},{2,3},{3,2},{4,5},{5,4},{6,7},{7,6},{8,9},{9,8},{10,11... | collective-permute-start | bytes 688136 | tf_op jit(solution)/shard_map/ppermute | solution.py:463

commit v3 on v2

--- a/solution.py
+++ b/solution.py
@@ -203,7 +203,10 @@
     source = lax.broadcasted_iota(jnp.int32, (rows, rows), 1)
     within = jnp.where(target < half, target, target - half)
     wanted_side = jnp.where(target < half, side, 1 - side)
-    origin = (within // tokens_in) * (2 * tokens_in) + wanted_side * tokens_in + within % tokens_in
+    zone = (within // tokens_in) % 2
+    member = within // (2 * tokens_in)
+    chip = zone * (half // (2 * tokens_in)) + member
+    origin = chip * (2 * tokens_in) + wanted_side * tokens_in + within % tokens_in
     sorter = jnp.where(source == origin, 1.0, 0.0).astype(jnp.bfloat16)
     ordered = jnp.dot(sorter, heads, preferred_element_type=jnp.float32).astype(jnp.bfloat16)
     own_ref[...] = ordered[:half]
@@ -270,21 +273,27 @@
     )(place(heads), place(flat_out), stay(up))
 
 
-def sum_kernel(keep_ref, other_ref, out_ref):
+def sum_kernel(zones, keep_ref, other_ref, out_ref):
     groups, rows, feature = out_ref.shape
+    members = groups // zones
     step = column_step(feature)
     for k in range(feature // step):
         columns = slice(k * step, (k + 1) * step)
         total = keep_ref[:, columns].astype(jnp.float32) + other_ref[:, columns].astype(
             jnp.float32
         )
-        out_ref[:, :, columns] = total.astype(jnp.bfloat16).reshape(groups, rows, step)
-
-
-def sum_halves(keep, other, groups):
+        total = total.astype(jnp.bfloat16).reshape(groups, rows, step)
+        if zones == 1:
+            out_ref[:, :, columns] = total
+        else:
+            for group in range(groups):
+                out_ref[group % zones * members + group // zones, :, columns] = total[group]
+
+
+def sum_halves(keep, other, groups, zones):
     count, feature = keep.shape
     return pl.pallas_call(
-        sum_kernel,
+        functools.partial(sum_kernel, zones),
         out_shape=jax.ShapeDtypeStruct((groups, count // groups, feature), jnp.bfloat16),
         in_specs=[VMEM_SPEC] * 2,
         out_specs=VMEM_SPEC,
@@ -292,47 +301,102 @@
     )(place(keep), place(other))
 
 
+def own_zone():
+    return lax.axis_index("ep") // (lax.axis_size("ep") // 2)
+
+
+def fold_kernel(shared_ref, residual_ref, ids_ref, part_ref, send_ref):
+    tokens, feature = residual_ref.shape
+    rows = 2 * tokens
+    mine = lax.broadcasted_iota(jnp.int32, (rows, 1), 0) // tokens == own_zone()
+    step = column_step(feature)
+    for k in range(feature // step):
+        columns = slice(k * step, (k + 1) * step)
+        part = jnp.sum(shared_ref[:, :, columns].astype(jnp.float32), axis=0)
+        residual = residual_ref[:, columns].astype(jnp.float32)
+        part = part + jnp.where(mine, jnp.concatenate([residual, residual], axis=0), 0.0)
+        part_ref[:, columns] = part
+        send_ref[:, columns] = part.astype(jnp.bfloat16)
+    ids = ids_ref[...].astype(jnp.float32)
+    ids = jnp.concatenate(
+        [ids, jnp.zeros((tokens, LANES - ids.shape[1]), jnp.float32)], axis=1
+    )
+    send_ref[:, feature:] = jnp.concatenate([ids, ids], axis=0).astype(jnp.bfloat16)
+
+
+def fold(shared, residual, expert_ids):
+    tokens, feature = residual.shape
+    return pl.pallas_call(
+        fold_kernel,
+        out_shape=[
+            jax.ShapeDtypeStruct((2 * tokens, feature), jnp.float32),
+            jax.ShapeDtypeStruct((2 * tokens, feature + LANES), jnp.bfloat16),
+        ],
+        in_specs=[VMEM_SPEC] * 3,
+        out_specs=[VMEM_SPEC] * 2,
+        compiler_params=pltpu.CompilerParams(vmem_limit_bytes=4 << 20),
+    )(place(shared), residual, expert_ids)
+
+
+def placed_slots(ids, expert, step_in_block, block_rows):
+    rows = ids.shape[0]
+    row = lax.broadcasted_iota(jnp.int32, (rows, expert.shape[1]), 0)
+    picked = jnp.zeros(row.shape, jnp.int32)
+    for k in range(ids.shape[1]):
+        picked = picked + jnp.where(ids[:, k : k + 1] == expert, 1, 0)
+    before = jnp.zeros(row.shape, jnp.int32)
+    for t in range(rows - 1):
+        later = (row > t) & (row // block_rows == t // block_rows)
+        before = before + jnp.where(later, picked[t : t + 1, :], 0)
+    return (picked > 0) & (before == step_in_block)
+
+
 def stream_kernel(
-    shared_ref,
-    residual_ref,
+    part_ref,
+    other_ref,
     gain_ref,
     ids_ref,
     share_ref,
     rows_ref,
     stream_ref,
     coefficient_ref,
+    total_ref,
 ):
-    tokens, feature = residual_ref.shape
-    experts, capacity, _ = rows_ref.shape
-    slots = coefficient_ref.shape[1]
+    rows, feature = part_ref.shape
+    tokens = rows // 2
+    members, zone_slots, _ = rows_ref.shape
+    capacity = zone_slots // 2
+    zone = own_zone()
     step = column_step(feature)
     blocks = [slice(k * step, (k + 1) * step) for k in range(feature // step)]
-    square = jnp.zeros((tokens, 1), jnp.float32)
+    square = jnp.zeros((rows, 1), jnp.float32)
     for columns in blocks:
-        attention = jnp.sum(shared_ref[:, :, columns].astype(jnp.float32), axis=0)
-        stream = residual_ref[:, columns].astype(jnp.float32) + attention
-        stream_ref[:, columns] = stream
-        square = square + jnp.sum(stream * stream, axis=1, keepdims=True)
+        total = part_ref[:, columns] + other_ref[:, columns].astype(jnp.float32)
+        total_ref[:, columns] = total
+        stream_ref[:, columns] = jnp.where(zone == 0, total[:tokens], total[tokens:])
+        square = square + jnp.sum(total * total, axis=1, keepdims=True)
     scale = lax.rsqrt(square / feature + norm_epsilon)
 
+    own_ids = ids_ref[...].astype(jnp.float32)
+    slots = coefficient_ref.shape[1]
     slot = lax.broadcasted_iota(jnp.int32, (tokens, slots), 1)
-    expert = slot // capacity
-    row = lax.broadcasted_iota(jnp.int32, (tokens, slots), 0)
-    picked = jnp.zeros((tokens, slots), jnp.int32)
+    expert = (slot // capacity).astype(jnp.float32)
     share = jnp.zeros((tokens, slots), jnp.float32)
     for k in range(ids_ref.shape[1]):
-        same = ids_ref[:, k : k + 1] == expert
-        picked = picked + jnp.where(same, 1, 0)
-        share = share + jnp.where(same, share_ref[:, k : k + 1], 0.0)
-    before = jnp.zeros((tokens, slots), jnp.int32)
-    for t in range(tokens - 1):
-        before = before + jnp.where(row > t, picked[t : t + 1, :], 0)
-    placed = (picked > 0) & (before == slot % capacity)
-    coefficient_ref[...] = jnp.where(placed, share, 0.0)
-    padded = jnp.concatenate(
-        [jnp.where(placed, 1.0, 0.0), jnp.zeros((8 - tokens, slots), jnp.float32)], axis=0
-    )
-    chooser = jnp.transpose(padded)[: experts * capacity].astype(jnp.bfloat16)
+        share = share + jnp.where(own_ids[:, k : k + 1] == expert, share_ref[:, k : k + 1], 0.0)
+    own_placed = placed_slots(own_ids, expert, slot % capacity, tokens)
+    coefficient_ref[...] = jnp.where(own_placed, share, 0.0)
+
+    width = -(-members * zone_slots // LANES) * LANES
+    row = lax.broadcasted_iota(jnp.int32, (rows, 1), 0)
+    other_ids = other_ref[:, feature : feature + ids_ref.shape[1]].astype(jnp.float32)
+    ids = jnp.where(row // tokens == zone, jnp.concatenate([own_ids, own_ids], axis=0), other_ids)
+    slot = lax.broadcasted_iota(jnp.int32, (rows, width), 1)
+    expert = (zone * members + slot // zone_slots).astype(jnp.float32)
+    placed = placed_slots(ids, expert, slot % capacity, tokens)
+    placed = placed & (slot // capacity % 2 == row // tokens)
+    chooser = jnp.transpose(jnp.where(placed, 1.0, 0.0))[: members * zone_slots]
+    chooser = chooser.astype(jnp.bfloat16)
     for columns in blocks:
         gain = jnp.concatenate(
             [
@@ -341,28 +405,33 @@
             ],
             axis=1,
         )
-        normed = stream_ref[:, columns] * scale * gain
-        normed = jnp.concatenate(
-            [normed, jnp.zeros((8 - tokens, step), jnp.float32)], axis=0
-        ).astype(jnp.bfloat16)
+        normed = (total_ref[:, columns] * scale * gain).astype(jnp.bfloat16)
         chosen = jnp.dot(chooser, normed, preferred_element_type=jnp.float32)
-        rows_ref[:, :, columns] = chosen.astype(jnp.bfloat16).reshape(experts, capacity, step)
-
-
-def route(shared, residual, gain, expert_ids, expert_weights, capacity):
-    experts, tokens, feature = shared.shape
+        rows_ref[:, :, columns] = chosen.astype(jnp.bfloat16).reshape(members, zone_slots, step)
+
+
+def route(part, other, gain, expert_ids, expert_weights, experts, capacity):
+    rows, feature = part.shape
+    tokens = rows // 2
     slots = -(-experts * capacity // LANES) * LANES
     return pl.pallas_call(
         stream_kernel,
         out_shape=[
-            jax.ShapeDtypeStruct((experts, capacity, feature), jnp.bfloat16),
+            jax.ShapeDtypeStruct((experts // 2, 2 * capacity, feature), jnp.bfloat16),
             jax.ShapeDtypeStruct((tokens, feature), jnp.float32),
             jax.ShapeDtypeStruct((tokens, slots), jnp.float32),
         ],
         in_specs=[VMEM_SPEC] * 5,
         out_specs=[VMEM_SPEC] * 3,
+        scratch_shapes=[pltpu.VMEM(part.shape, jnp.float32)],
         compiler_params=pltpu.CompilerParams(vmem_limit_bytes=4 << 20),
-    )(place(shared), residual, gain.reshape(feature // LANES, LANES), expert_ids, expert_weights)
+    )(
+        place(part),
+        place(other),
+        gain.reshape(feature // LANES, LANES),
+        expert_ids,
+        expert_weights,
+    )
 
 
 def mix_kernel(returned_ref, coefficient_ref, stream_ref, out_ref):
@@ -399,64 +468,88 @@
     )(place(returned), place(coefficient), place(stream))
 
 
-def expert_kernel(
-    own_rows_ref,
-    other_rows_ref,
-    gate_ref,
-    up_ref,
-    down_hbm,
-    keep_ref,
-    send_ref,
-    down_ref,
-    hidden_ref,
-    sem,
-):
-    load = pltpu.make_async_copy(down_hbm, down_ref, sem)
-    load.start()
+def fill_hidden(rows, gate_ref, up_ref, hidden_ref):
     width = gate_ref.shape[1]
-    feature = down_hbm.shape[1]
-    hidden_step = 256 if width % 256 == 0 else width
-    step = column_step(feature)
-    shape = own_rows_ref.shape
-    own_count = shape[0] * shape[1]
-    rows = jnp.concatenate(
-        [
-            own_rows_ref[...].reshape(own_count, shape[2]),
-            other_rows_ref[...].reshape(own_count, shape[2]),
-        ]
-    )
-    for k in range(width // hidden_step):
-        columns = slice(k * hidden_step, (k + 1) * hidden_step)
+    step = 256 if width % 256 == 0 else width
+    for k in range(width // step):
+        columns = slice(k * step, (k + 1) * step)
         gate_part = jnp.dot(rows, gate_ref[:, columns], preferred_element_type=jnp.float32)
         up_part = jnp.dot(rows, up_ref[:, columns], preferred_element_type=jnp.float32)
         hidden_ref[:, columns] = (gate_part / (1.0 + jnp.exp(-gate_part)) * up_part).astype(
             jnp.bfloat16
         )
-    hidden = hidden_ref[...]
+
+
+def fill_partial(hidden, down_ref, out_ref):
+    step = column_step(down_ref.shape[1])
+    for k in range(down_ref.shape[1] // step):
+        columns = slice(k * step, (k + 1) * step)
+        out_ref[:, columns] = jnp.dot(
+            hidden, down_ref[:, columns], preferred_element_type=jnp.float32
+        ).astype(jnp.bfloat16)
+
+
+def own_hidden_kernel(rows_ref, gate_ref, up_ref, down_hbm, hidden_ref, down_ref, sem):
+    load = pltpu.make_async_copy(down_hbm, down_ref, sem)
+    load.start()
+    shape = rows_ref.shape
+    rows = rows_ref[...].reshape(shape[0] * shape[1], shape[2])
+    fill_hidden(rows, gate_ref, up_ref, hidden_ref)
     load.wait()
-    for k in range(feature // step):
-        columns = slice(k * step, (k + 1) * step)
-        out = jnp.dot(hidden, down_ref[:, columns], preferred_element_type=jnp.float32).astype(
-            jnp.bfloat16
-        )
-        keep_ref[:, columns] = out[:own_count]
-        send_ref[:, columns] = out[own_count:]
-
-
-def expert_halves(own_rows, other_rows, gate, up, down):
-    count, feature = own_rows.shape[0] * own_rows.shape[1], own_rows.shape[2]
-    return pl.pallas_call(
-        expert_kernel,
-        out_shape=[jax.ShapeDtypeStruct((count, feature), jnp.bfloat16)] * 2,
-        in_specs=[VMEM_SPEC] * 4 + [HBM_SPEC],
+
+
+def own_hidden(rows, gate, up, down):
+    count = rows.shape[0] * rows.shape[1]
+    return pl.pallas_call(
+        own_hidden_kernel,
+        out_shape=[
+            jax.ShapeDtypeStruct((count, gate.shape[1]), jnp.bfloat16),
+            pltpu.VMEM(down.shape, down.dtype),
+        ],
+        in_specs=[VMEM_SPEC] * 3 + [HBM_SPEC],
         out_specs=[VMEM_SPEC] * 2,
-        scratch_shapes=[
-            pltpu.VMEM(down.shape, down.dtype),
-            pltpu.VMEM((2 * count, gate.shape[1]), jnp.bfloat16),
-            pltpu.SemaphoreType.DMA,
-        ],
-        compiler_params=pltpu.CompilerParams(vmem_limit_bytes=16 << 20),
-    )(place(own_rows), place(other_rows), place(gate), place(up), stay(down))
+        scratch_shapes=[pltpu.SemaphoreType.DMA],
+        compiler_params=pltpu.CompilerParams(vmem_limit_bytes=8 << 20),
+        cost_estimate=pl.CostEstimate(
+            flops=4 * count * gate.size, bytes_accessed=6 * gate.size, transcendentals=0
+        ),
+    )(place(rows), place(gate), place(up), stay(down))
+
+
+def other_partial_kernel(rows_ref, gate_ref, up_ref, down_ref, send_ref, hidden_ref):
+    shape = rows_ref.shape
+    rows = rows_ref[...].reshape(shape[0] * shape[1], shape[2])
+    fill_hidden(rows, gate_ref, up_ref, hidden_ref)
+    fill_partial(hidden_ref[...], down_ref, send_ref)
+
+
+def other_partial(rows, gate, up, down):
+    count, feature = rows.shape[0] * rows.shape[1], rows.shape[2]
+    return pl.pallas_call(
+        other_partial_kernel,
+        out_shape=jax.ShapeDtypeStruct((count, feature), jnp.bfloat16),
+        in_specs=[VMEM_SPEC] * 4,
+        out_specs=VMEM_SPEC,
+        scratch_shapes=[pltpu.VMEM((count, gate.shape[1]), jnp.bfloat16)],
+        compiler_params=pltpu.CompilerParams(vmem_limit_bytes=8 << 20),
+    )(place(rows), place(gate), place(up), place(down))
+
+
+def own_partial_kernel(hidden_ref, down_ref, keep_ref):
+    fill_partial(hidden_ref[...], down_ref, keep_ref)
+
+
+def own_partial(hidden, down):
+    return pl.pallas_call(
+        own_partial_kernel,
+        out_shape=jax.ShapeDtypeStruct((hidden.shape[0], down.shape[1]), jnp.bfloat16),
+        in_specs=[VMEM_SPEC] * 2,
+        out_specs=VMEM_SPEC,
+        compiler_params=pltpu.CompilerParams(vmem_limit_bytes=4 << 20),
+        cost_estimate=pl.CostEstimate(
+            flops=2 * hidden.shape[0] * down.size, bytes_accessed=2 * down.size, transcendentals=0
+        ),
+    )(place(hidden), place(down))
 
 
 def swap_sides(block):
@@ -482,7 +575,7 @@
     feature = residual.shape[1]
     ep_count = lax.axis_size("ep")
     side_count = lax.axis_size("side")
-    assert side_count == 2
+    assert side_count == 2 and ep_count % 2 == 0 and ep_count <= 256
     flat_out = output_proj.reshape(output_proj.shape[0] * output_proj.shape[1], feature)
     capacity = min(
         row_count, max(2, (row_count * expert_ids.shape[1] + ep_count - 1) // ep_count)
@@ -495,15 +588,28 @@
     send, own_heads, gate = project_heads(arrived, value_up, flat_out, gate_proj[0])
     from_other = swap_sides(send)
     keep, up = project_own(own_heads, flat_out, up_proj[0])
-    contribution = sum_halves(keep, from_other, ep_count)
-    shared = lax.all_to_all(contribution, "ep", split_axis=0, concat_axis=0, tiled=True)
+    members = ep_count // 2
+    zones = [list(range(members)), list(range(members, ep_count))]
+    contribution = sum_halves(keep, from_other, members, 1)
+    shared = lax.all_to_all(
+        contribution, "ep", split_axis=0, concat_axis=0, tiled=True, axis_index_groups=zones
+    )
+    part, part_copy = fold(shared, residual, expert_ids)
+    other_part = lax.ppermute(
+        part_copy, "ep", [(e, (e + members) % ep_count) for e in range(ep_count)]
+    )
     outbound, stream, coefficient = route(
-        shared, residual, norm_gain, expert_ids, expert_weights, capacity
-    )
-    own_rows = lax.all_to_all(outbound, "ep", split_axis=0, concat_axis=0, tiled=True)
+        part, other_part, norm_gain, expert_ids, expert_weights, ep_count, capacity
+    )
+    own_rows = lax.all_to_all(
+        outbound, "ep", split_axis=0, concat_axis=0, tiled=True, axis_index_groups=zones
+    )
     other_rows = swap_sides(own_rows)
-    keep, send = expert_halves(own_rows, other_rows, gate, up, down_proj[0])
-    both = sum_halves(keep, swap_sides(send), ep_count)
+    hidden, down = own_hidden(own_rows, gate, up, down_proj[0])
+    send = other_partial(other_rows, gate, up, down)
+    other = swap_sides(send)
+    keep = own_partial(hidden, down)
+    both = sum_halves(keep, other, ep_count, 2)
     returned = lax.all_to_all(both, "ep", split_axis=0, concat_axis=0, tiled=True)
     return mix(returned, coefficient, stream)
 

time: 82.1 us -> 77.1 us (0.939)
  blocking collectives: 66.1 us -> 56.6 us
  waiting for transfers between devices: 2.84 us -> 4.72 us
  starting transfers between devices: 0.27 us -> 2.1 us
    all_to_all x2, blocking collectives: 30.2 us -> 21.2 us  [the longest x1 12.3 us: local(): lax.all_to_all(contribution, 'ep', split_axis=0, concat_axis=0, tiled=Tru...]
    ppermute x0 -> x1, waiting for transfers between devices: none -> 4.32 us  [local(): lax.ppermute(part_copy, 'ep', [(e, (e + members) % ep_count) for e in ran...]
    ppermute x3, waiting for transfers between devices: 2.84 us -> 0.4 us  [swap_sides(): return lax.ppermute(block, 'side', [(0, 1), (1, 0)])]
    ppermute x0 -> x1, starting transfers between devices: none -> 1.48 us  [local(): lax.ppermute(part_copy, 'ep', [(e, (e + members) % ep_count) for e in ran...]
    pallas_call x4 -> x7, Pallas kernels: 4.69 us -> 5.41 us  [the longest x1 2.05 us: own_hidden(): pl.pallas_call(own_hidden_kernel, out_shape=[jax.ShapeDtypeStruct((count,...]
  transfers between devices with their start and end apart: 3 -> 4, of which waited for: 2 -> 2; matrix products, arithmetic and copies ran while one was open for 0% -> 0% of each run, Pallas kernels for 3% -> 6%
where the time goes in v3:
time: 77.1 us; the launch traced here: 76.8 us
  blocking collectives  56.6 us (73%)
  Pallas kernels  13.2 us (17%)
  waiting for transfers between devices  4.72 us (6%)
  starting transfers between devices  2.1 us (3%)
    all_to_all x1, blocking collectives, local(): lax.all_to_all(latent, ('ep', 'side'), split_axis=0, concat_axis=0, tiled...  22.7 us
    all_to_all x1, blocking collectives, local(): lax.all_to_all(both, 'ep', split_axis=0, concat_axis=0, tiled=True)  12.6 us
    all_to_all x1, blocking collectives, local(): lax.all_to_all(contribution, 'ep', split_axis=0, concat_axis=0, tiled=Tru...  12.3 us
    all_to_all x1, blocking collectives, local(): lax.all_to_all(outbound, 'ep', split_axis=0, concat_axis=0, tiled=True, a...  8.9 us
    ppermute x1, waiting for transfers between devices, local(): lax.ppermute(part_copy, 'ep', [(e, (e + members) % ep_count) for e in ran...  4.32 us
    pallas_call x1, Pallas kernels, attend(): pl.pallas_call(attention_kernel, out_shape=[jax.ShapeDtypeStruct((holders...  2.91 us
    pallas_call x1, Pallas kernels, project_own(): pl.pallas_call(own_kernel, out_shape=[jax.ShapeDtypeStruct((rows, feature...  2.07 us
    pallas_call x1, Pallas kernels, own_hidden(): pl.pallas_call(own_hidden_kernel, out_shape=[jax.ShapeDtypeStruct((count,...  2.05 us
  transfers between devices with their start and end apart: 4, of which 2 were waited for; matrix products, arithmetic and copies ran while one was open for 0% of the time, Pallas kernels for 6%

profile of v3, /device:TPU:0, one launch (start us, length us, event | category | flops | bytes accessed | tf_op | source)
XLA Modules:
  0.0 76.8 jit_solution(3323232996695832374)
XLA Ops:
  0.0 2.9 %shard_map.127 = (bf16[32,16,512]{2,1,0:T(8,128)(2,1)S(1)}, bf16[4,512,128]{2,1,0:T(8,128)(2,1)S(1)}, bf16[512,3584]{1,0:T(8,128)(2,1)S(1)}) custom-call(s32[2]{0:T(128)} %lengths_hbm.1, bf16[4,576,128]{2,1,0:T(8,128)(2,1)} %bitcast.12, bf16[2,576,128]{2,1,0:T(8,128)(2,1)} %bitcast.13, bf16[4,576]{1,0:T(4,128)(2,1)} %fresh_hbm.1, ...), custom_call_target="tpu_custom_call" | custom-call | tf_op jit(solution)/shard_map/pallas_call | solution.py:142
  2.9 22.7 %all_to_all.20.arrived_ref = bf16[32,16,512]{2,1,0:T(8,128)(2,1)S(1)} all-to-all(bf16[32,16,512]{2,1,0:T(8,128)(2,1)S(1)} %get-tuple-element.20), channel_id=1, replica_groups=mesh['groups'=1,'ep'=16,'side'=2] {'ep','side'}, dimensions={0} | all-to-all | bytes 1048576 | tf_op jit(solution)/shard_map/all_to_all | solution.py:587
  25.7 2.0 %shard_map.128 = (bf16[64,3584]{1,0:T(8,128)(2,1)S(1)}, bf16[64,512]{1,0:T(8,128)(2,1)S(1)}, bf16[3584,512]{1,0:T(8,128)(2,1)S(1)}) custom-call(bf16[32,16,512]{2,1,0:T(8,128)(2,1)S(1)} %all_to_all.20.arrived_ref, bf16[4,512,128]{2,1,0:T(8,128)(2,1)S(1)} %get-tuple-element.21.up_ref, bf16[512,3584]{1,0:T(8,128)(2,1)S(1)} %get-tuple-element.22.out_ref, ...), custom_call_target="tpu_custom_call" | custom-call | tf_op jit(solution)/shard_map/pallas_call | solution.py:227
  27.7 0.1 collective-permute-start
  27.8 0.0 copy-start
  27.8 0.0 copy-start.2
  27.8 0.0 copy-start.1
  27.8 0.0 copy-start.3
  27.8 2.1 %shard_map.129 = (f32[64,3584]{1,0:T(8,128)S(1)}, bf16[3584,512]{1,0:T(8,128)(2,1)S(1)}) custom-call(bf16[64,512]{1,0:T(8,128)(2,1)S(1)} %get-tuple-element.23.heads_ref, bf16[512,3584]{1,0:T(8,128)(2,1)S(1)} %get-tuple-element.22.out_ref, bf16[3584,512]{1,0:T(8,128)(2,1)} %bitcast.9), custom_call_target="tpu_custom_call" | custom-call | flops 234881024 | bytes 7340032 | tf_op jit(solution)/shard_map/pallas_call | solution.py:258
  29.9 0.0 collective-permute-done.other_ref
  29.9 0.1 shard_map.130
  30.0 12.3 %all_to_all.21.shared_ref = bf16[8,8,3584]{2,1,0:T(8,128)(2,1)S(1)} all-to-all(bf16[8,8,3584]{2,1,0:T(8,128)(2,1)S(1)} %shard_map.130), channel_id=1, replica_groups={{0,2,4,6,8,10,12,14},{16,18,20,22,24,26,28,30},{1,3,5,7,9,11,13,15},{17..., dimensions={0} | all-to-all | bytes 917504 | tf_op jit(solution)/shard_map/all_to_all | solution.py:594
  42.3 0.0 copy-done
  42.3 0.0 copy-done.2
  42.3 0.1 shard_map.131
  42.4 1.5 %collective-permute-start.1 = (bf16[8,3712]{1,0:T(8,128)(2,1)S(1)}, bf16[8,3712]{1,0:T(8,128)(2,1)S(1)}, u32[]{:S(2)}, u32[]{:S(2)}) collective-permute-start(bf16[8,3712]{1,0:T(8,128)(2,1)S(1)} %get-tuple-element.27), channel_id=1, source_target_pairs={{0,16},{2,18},{4,20},{6,22},{8,24},{10,26},{12,28},{14,30},{16,0},... | collective-permute-start | bytes 178184 | tf_op jit(solution)/shard_map/ppermute | solution.py:598
  43.9 4.3 %collective-permute-done.1.other_ref = bf16[8,3712]{1,0:T(8,128)(2,1)S(1)} collective-permute-done((bf16[8,3712]{1,0:T(8,128)(2,1)S(1)}, bf16[8,3712]{1,0:T(8,128)(2,1)S(1)}, u32[]{:S(2)}, u32[]{:S(2)}) %collective-permute-start.1) | collective-permute-done | bytes 59424 | tf_op jit(solution)/shard_map/ppermute | solution.py:598
  48.2 0.0 copy-done.1
  48.2 0.0 copy-done.3
  48.2 0.4 shard_map.132
  48.6 8.9 %all_to_all.22.rows_ref = bf16[8,4,3584]{2,1,0:T(4,128)(2,1)S(1)} all-to-all(bf16[8,4,3584]{2,1,0:T(4,128)(2,1)S(1)} %get-tuple-element.28), channel_id=1, replica_groups={{0,2,4,6,8,10,12,14},{16,18,20,22,24,26,28,30},{1,3,5,7,9,11,13,15},{17..., dimensions={0} | all-to-all | bytes 458752 | tf_op jit(solution)/shard_map/all_to_all | solution.py:604
  57.5 0.0 collective-permute-start.2
  57.5 2.0 %shard_map.133 = (bf16[32,512]{1,0:T(8,128)(2,1)S(1)}, bf16[512,3584]{1,0:T(8,128)(2,1)S(1)}) custom-call(bf16[8,4,3584]{2,1,0:T(4,128)(2,1)S(1)} %all_to_all.22.rows_ref, bf16[3584,512]{1,0:T(8,128)(2,1)S(1)} %get-tuple-element.29.gate_ref, bf16[3584,512]{1,0:T(8,128)(2,1)S(1)} %get-tuple-element.30.up_ref, bf16[512,3584]{1,0:T(8,128)(2,1)} %bitcast.11), custom_call_target="tpu_custom_call" | custom-call | flops 234881024 | bytes 11010048 | tf_op jit(solution)/shard_map/pallas_call | solution.py:503
  59.5 0.0 collective-permute-done.2.rows_ref
  59.5 2.0 %shard_map.135 = bf16[32,3584]{1,0:T(8,128)(2,1)S(1)} custom-call(bf16[8,4,3584]{2,1,0:T(4,128)(2,1)S(1)} %collective-permute-done.2.rows_ref, bf16[3584,512]{1,0:T(8,128)(2,1)S(1)} %get-tuple-element.29.gate_ref, bf16[3584,512]{1,0:T(8,128)(2,1)S(1)} %get-tuple-element.30.up_ref, bf16[512,3584]{1,0:T(8,128)(2,1)S(1)} %get-tuple-element.32.down_ref), custom_call_target="tpu_custom_call" | custom-call | tf_op jit(solution)/shard_map/pallas_call | solution.py:528
  61.6 0.5 collective-permute-start.3
  62.1 0.7 shard_map.134.keep_ref
  62.8 0.4 collective-permute-done.3.other_ref
  63.2 0.1 shard_map.136
  63.3 12.6 %all_to_all.23.returned_ref = bf16[16,2,3584]{2,1,0:T(2,128)(2,1)S(1)} all-to-all(bf16[16,2,3584]{2,1,0:T(2,128)(2,1)S(1)} %shard_map.136), channel_id=1, replica_groups=mesh['groups'=1,'ep'=16,'side'=2] {'ep'}, dimensions={0} | all-to-all | bytes 458752 | tf_op jit(solution)/shard_map/all_to_all | solution.py:613
  76.0 0.8 %shard_map.137 = bf16[4,3584]{1,0:T(4,128)(2,1)} custom-call(bf16[16,2,3584]{2,1,0:T(2,128)(2,1)S(1)} %all_to_all.23.returned_ref, f32[4,128]{1,0:T(4,128)S(1)} %get-tuple-element.33.coefficient_ref, f32[4,3584]{1,0:T(4,128)S(1)} %get-tuple-element.34.stream_ref), custom_call_target="tpu_custom_call" | custom-call | tf_op jit(solution)/shard_map/pallas_call | solution.py:462
Async XLA Ops:
  27.7 2.2 %collective-permute-start = (bf16[64,3584]{1,0:T(8,128)(2,1)S(1)}, bf16[64,3584]{1,0:T(8,128)(2,1)S(1)}, u32[]{:S(2)}, u32[]{:S(2)}) collective-permute-start(bf16[64,3584]{1,0:T(8,128)(2,1)S(1)} %get-tuple-element.25), channel_id=1, source_target_pairs={{0,1},{1,0},{2,3},{3,2},{4,5},{5,4},{6,7},{7,6},{8,9},{9,8},{10,11... | collective-permute-start | bytes 1376264 | tf_op jit(solution)/shard_map/ppermute | solution.py:556
  27.8 14.5 %copy-start = (bf16[4,3584]{1,0:T(4,128)(2,1)S(1)}, bf16[4,3584]{1,0:T(4,128)(2,1)}, u32[]{:S(2)}) copy-start(bf16[4,3584]{1,0:T(4,128)(2,1)} %residual_ref.1) | copy-start | bytes 86020
  27.8 14.5 %copy-start.2 = (s32[4,8]{1,0:T(4,128)S(1)}, s32[4,8]{1,0:T(4,128)}, u32[]{:S(2)}) copy-start(s32[4,8]{1,0:T(4,128)} %ids_ref.3) | copy-start | bytes 388
  27.8 20.4 %copy-start.1 = (f32[3584]{0:T(1024)S(1)}, f32[3584]{0:T(1024)}, u32[]{:S(2)}) copy-start(f32[3584]{0:T(1024)} %param.18) | copy-start | bytes 43012
  27.8 20.4 %copy-start.3 = (f32[4,8]{1,0:T(4,128)S(1)}, f32[4,8]{1,0:T(4,128)}, u32[]{:S(2)}) copy-start(f32[4,8]{1,0:T(4,128)} %share_ref.1) | copy-start | bytes 388
  42.4 5.8 %collective-permute-start.1 = (bf16[8,3712]{1,0:T(8,128)(2,1)S(1)}, bf16[8,3712]{1,0:T(8,128)(2,1)S(1)}, u32[]{:S(2)}, u32[]{:S(2)}) collective-permute-start(bf16[8,3712]{1,0:T(8,128)(2,1)S(1)} %get-tuple-element.27), channel_id=1, source_target_pairs={{0,16},{2,18},{4,20},{6,22},{8,24},{10,26},{12,28},{14,30},{16,0},... | collective-permute-start | bytes 178184 | tf_op jit(solution)/shard_map/ppermute | solution.py:598
  57.5 2.1 %collective-permute-start.2 = (bf16[8,4,3584]{2,1,0:T(4,128)(2,1)S(1)}, bf16[8,4,3584]{2,1,0:T(4,128)(2,1)S(1)}, u32[]{:S(2)}, u32[]{:S(2)}) collective-permute-start(bf16[8,4,3584]{2,1,0:T(4,128)(2,1)S(1)} %all_to_all.22.rows_ref), channel_id=1, source_target_pairs={{0,1},{1,0},{2,3},{3,2},{4,5},{5,4},{6,7},{7,6},{8,9},{9,8},{10,11... | collective-permute-start | bytes 688136 | tf_op jit(solution)/shard_map/ppermute | solution.py:556
  61.6 1.7 %collective-permute-start.3 = (bf16[32,3584]{1,0:T(8,128)(2,1)S(1)}, bf16[32,3584]{1,0:T(8,128)(2,1)S(1)}, u32[]{:S(2)}, u32[]{:S(2)}) collective-permute-start(bf16[32,3584]{1,0:T(8,128)(2,1)S(1)} %shard_map.135), channel_id=1, source_target_pairs={{0,1},{1,0},{2,3},{3,2},{4,5},{5,4},{6,7},{7,6},{8,9},{9,8},{10,11... | collective-permute-start | bytes 688136 | tf_op jit(solution)/shard_map/ppermute | solution.py:556

commit v4 on v3

--- a/solution.py
+++ b/solution.py
@@ -25,6 +25,18 @@
 
 def place(array):
     return pltpu.with_memory_space_constraint(array, pltpu.VMEM)
+
+
+def column_step(width):
+    for step in (512, 384, 256, 128):
+        if width % step == 0:
+            return step
+    return width
+
+
+def left_columns(width):
+    step = column_step(width)
+    return width // step * 3 // 4 * step
 
 
 def attention_kernel(
@@ -41,8 +53,6 @@
     queries_ref,
     cache_ref,
     fresh_ref,
-    rows_ref,
-    placed_ref,
     sems,
 ):
     requests = cache_hbm.shape[0]
@@ -65,71 +75,72 @@
     count = 2 + 2 * requests
     loads = [
         pltpu.make_async_copy(up_hbm, up_ref, sems.at[count]),
-        pltpu.make_async_copy(project_hbm, project_ref, sems.at[count + 1]),
+        pltpu.make_async_copy(
+            project_hbm.at[:, : project_ref.shape[1]], project_ref, sems.at[count + 1]
+        ),
     ]
     for copy in first + sum(pieces, []) + loads:
         copy.start()
-    for copy in first:
+    factor = 1.0 / QKD**0.5
+    context = cache_ref.shape[2]
+    heads = queries_ref.shape[2]
+    holders, block, latent_width = out_ref.shape
+    rows = block // requests
+    own_heads = rows // positions
+    extra = 16
+    width = positions * heads
+    target = lax.broadcasted_iota(jnp.int32, (width, width), 0)
+    source = lax.broadcasted_iota(jnp.int32, (width, width), 1)
+    origin = (
+        (target % rows) // own_heads * heads + target // rows * own_heads + target % own_heads
+    )
+    sorter = jnp.where(source == origin, 1.0, 0.0).astype(jnp.bfloat16)
+    row = lax.broadcasted_iota(jnp.int32, (context + extra, width), 0)
+    step = lax.broadcasted_iota(jnp.int32, (context + extra, width), 1) // heads
+    fresh_live = (row >= context) & (row - context <= step)
+    tail_row = lax.broadcasted_iota(jnp.int32, (extra, width), 0)
+    key_row = lax.broadcasted_iota(jnp.int32, (context + extra, LANES), 0)
+    scale_columns = jnp.where(
+        (key_row >= context + positions) & (key_row < context + positions + 3), 1.0, 0.0
+    ).astype(jnp.bfloat16)
+    for copy in first + sum(pieces, []):
         copy.wait()
-    factor = 1.0 / QKD**0.5
-    tokens, _, heads = queries_ref.shape
-    holders, block, latent_width = out_ref.shape
-    own_heads = block // tokens
-    fresh_rows = -(-positions // 8) * 8
     for r in range(requests):
-        for copy in pieces[r]:
-            copy.wait()
-        keys = jnp.transpose(cache_ref[r])
+        fresh = fresh_ref[r * positions : (r + 1) * positions, :]
+        keys = jnp.concatenate(
+            [
+                jnp.transpose(cache_ref[r]),
+                fresh,
+                jnp.zeros((extra - positions, fresh.shape[1]), fresh.dtype),
+            ],
+            axis=0,
+        )
         wanted = jnp.concatenate(
             [queries_ref[r * positions + j] for j in range(positions)], axis=1
         )
-        fresh = fresh_ref[r * positions : (r + 1) * positions, :]
-        cache_scores = jnp.dot(keys, wanted, preferred_element_type=jnp.float32) * factor
-        padded = jnp.concatenate(
-            [fresh, jnp.zeros((16 - positions, fresh.shape[1]), fresh.dtype)], axis=0
-        )
-        fresh_scores = (
-            jnp.dot(padded, wanted, preferred_element_type=jnp.float32)[:fresh_rows] * factor
-        )
-        cache_live = lax.broadcasted_iota(jnp.int32, cache_scores.shape, 0) < lengths_ref[r]
-        fresh_row = lax.broadcasted_iota(jnp.int32, fresh_scores.shape, 0)
-        step = lax.broadcasted_iota(jnp.int32, fresh_scores.shape, 1) // heads
-        fresh_live = fresh_row <= step
-        cache_scores = jnp.where(cache_live, cache_scores, masked_score)
-        fresh_scores = jnp.where(fresh_live, fresh_scores, masked_score)
-        highest = jnp.maximum(
-            jnp.max(cache_scores, axis=0, keepdims=True),
-            jnp.max(fresh_scores, axis=0, keepdims=True),
-        )
-        cache_weight = jnp.where(cache_live, jnp.exp(cache_scores - highest), 0.0)
-        fresh_weight = jnp.where(fresh_live, jnp.exp(fresh_scores - highest), 0.0)
-        total = jnp.sum(cache_weight, axis=0, keepdims=True) + jnp.sum(
-            fresh_weight, axis=0, keepdims=True
-        )
-        side_columns = jnp.where(fresh_row == positions, total, fresh_weight)
-        for j in range(positions):
-            lanes = slice(j * heads, (j + 1) * heads)
-            columns = jnp.transpose(side_columns[:, lanes])
-            weights = jnp.transpose(cache_weight[:, lanes]).astype(jnp.bfloat16)
-            merged = jnp.dot(
-                weights, keys[:, :latent_width], preferred_element_type=jnp.float32
+        scores = jnp.dot(keys, wanted, preferred_element_type=jnp.float32) * factor
+        live = (row < lengths_ref[r]) | fresh_live
+        scores = jnp.where(live, scores, masked_score)
+        highest = jnp.max(scores, axis=0, keepdims=True)
+        weights = jnp.where(live, jnp.exp(scores - highest), 0.0)
+        inverse = 1.0 / jnp.sum(weights, axis=0, keepdims=True)
+        tail = weights[context:]
+        for n in range(3):
+            term = inverse.astype(jnp.bfloat16).astype(jnp.float32)
+            inverse = inverse - term
+            tail = jnp.where(tail_row == positions + n, term, tail)
+        weights = jnp.concatenate([weights[:context], tail], axis=0).astype(jnp.bfloat16)
+        ordered = lax.dot_general(
+            sorter, weights, (((1,), (1,)), ((), ())), preferred_element_type=jnp.float32
+        )
+        ordered = ordered.astype(jnp.bfloat16)
+        scale = jnp.dot(ordered, scale_columns, preferred_element_type=jnp.float32)
+        merged = jnp.dot(ordered, keys[:, :latent_width], preferred_element_type=jnp.float32)
+        for part in range(latent_width // LANES):
+            columns = slice(part * LANES, (part + 1) * LANES)
+            out_ref[:, r * rows : (r + 1) * rows, columns] = (
+                (merged[:, columns] * scale).astype(jnp.bfloat16).reshape(holders, rows, LANES)
             )
-            for q in range(j + 1):
-                merged = merged + columns[:, q : q + 1].astype(jnp.bfloat16).astype(
-                    jnp.float32
-                ) * fresh[q : q + 1, :latent_width].astype(jnp.float32)
-            merged = merged / columns[:, positions : positions + 1]
-            token = r * positions + j
-            for part in range(latent_width // LANES):
-                rows_ref[part] = merged[:, part * LANES : (part + 1) * LANES]
-                for i in range(own_heads):
-                    placed_ref[part, pl.ds(token * own_heads + i, holders, stride=block), :] = (
-                        rows_ref[part, pl.ds(i, holders, stride=own_heads), :]
-                    )
-    for part in range(latent_width // LANES):
-        out_ref[:, :, part * LANES : (part + 1) * LANES] = (
-            placed_ref[part].astype(jnp.bfloat16).reshape(holders, block, LANES)
-        )
     for copy in loads:
         copy.wait()
 
@@ -144,63 +155,45 @@
         out_shape=[
             jax.ShapeDtypeStruct((holders, block, LAT), jnp.bfloat16),
             pltpu.VMEM(value_up.shape, value_up.dtype),
-            pltpu.VMEM(flat_out.shape, flat_out.dtype),
+            pltpu.VMEM((flat_out.shape[0], left_columns(flat_out.shape[1])), flat_out.dtype),
         ],
         in_specs=[HBM_SPEC] * 6,
         out_specs=[VMEM_SPEC] * 3,
         scratch_shapes=[pltpu.SMEM(lengths.shape, lengths.dtype)]
         + [pltpu.VMEM(x.shape, x.dtype) for x in operands[1:]]
-        + [
-            pltpu.VMEM((LAT // LANES, heads, LANES), jnp.float32),
-            pltpu.VMEM((LAT // LANES, tokens * heads, LANES), jnp.float32),
-            pltpu.SemaphoreType.DMA((4 + 2 * requests,)),
-        ],
+        + [pltpu.SemaphoreType.DMA((4 + 2 * requests,))],
         compiler_params=pltpu.CompilerParams(vmem_limit_bytes=16 << 20),
     )(*map(stay, operands + (value_up, flat_out)))
 
 
-def column_step(width):
-    for step in (512, 384, 256, 128):
-        if width % step == 0:
-            return step
-    return width
+def project_columns(rows, weight_ref, out_ref, start):
+    step = column_step(weight_ref.shape[1])
+    for k in range(weight_ref.shape[1] // step):
+        out_ref[:, start + k * step : start + (k + 1) * step] = jnp.dot(
+            rows, weight_ref[:, k * step : (k + 1) * step], preferred_element_type=jnp.float32
+        ).astype(out_ref.dtype)
 
 
 def head_kernel(
-    arrived_ref, up_ref, out_ref, gate_hbm, send_ref, own_ref, gate_ref, wide_ref, sem
+    arrived_ref, up_ref, left_ref, out_hbm, send_ref, own_ref, right_ref, sem
 ):
-    load = pltpu.make_async_copy(gate_hbm, gate_ref, sem)
+    load = pltpu.make_async_copy(out_hbm.at[:, left_ref.shape[1] :], right_ref, sem)
     load.start()
     tokens_in = arrived_ref.shape[1] // up_ref.shape[0]
     sources, block, latent_width = arrived_ref.shape
     own_heads, _, value_width = up_ref.shape
-    step = column_step(out_ref.shape[1])
-    steps = out_ref.shape[1] // step
     rows = sources * tokens_in
-    parts = latent_width // LANES
-    for part in range(parts):
-        wide_ref[part] = (
-            arrived_ref[:, :, part * LANES : (part + 1) * LANES]
-            .reshape(sources * block, LANES)
-            .astype(jnp.float32)
-        )
+    latent = arrived_ref[...].reshape(sources * block, latent_width)
+    head = lax.broadcasted_iota(jnp.int32, (sources * block, value_width), 0) % own_heads
     outs = []
     for i in range(own_heads):
-        latent = jnp.concatenate(
-            [
-                wide_ref[part, pl.ds(i, rows, stride=own_heads), :].astype(jnp.bfloat16)
-                for part in range(parts)
-            ],
-            axis=1,
-        )
-        outs.append(
-            jnp.dot(latent, up_ref[i], preferred_element_type=jnp.float32).astype(jnp.bfloat16)
-        )
+        out = jnp.dot(latent, up_ref[i], preferred_element_type=jnp.float32)
+        outs.append(jnp.where(head == i, out, 0.0).astype(jnp.bfloat16))
     heads = jnp.concatenate(outs, axis=1)
     side = lax.axis_index("side")
     half = rows // 2
-    target = lax.broadcasted_iota(jnp.int32, (rows, rows), 0)
-    source = lax.broadcasted_iota(jnp.int32, (rows, rows), 1)
+    target = lax.broadcasted_iota(jnp.int32, (rows, rows * own_heads), 0)
+    source = lax.broadcasted_iota(jnp.int32, (rows, rows * own_heads), 1) // own_heads
     within = jnp.where(target < half, target, target - half)
     wanted_side = jnp.where(target < half, side, 1 - side)
     zone = (within // tokens_in) % 2
@@ -211,66 +204,74 @@
     ordered = jnp.dot(sorter, heads, preferred_element_type=jnp.float32).astype(jnp.bfloat16)
     own_ref[...] = ordered[:half]
     other = ordered[half:]
-    for k in range(steps):
-        columns = slice(k * step, (k + 1) * step)
-        send_ref[:, columns] = jnp.dot(
-            other, out_ref[:, columns], preferred_element_type=jnp.float32
-        ).astype(jnp.bfloat16)
+    project_columns(other, left_ref, send_ref, 0)
     load.wait()
-
-
-def project_heads(arrived, value_up, flat_out, gate):
+    project_columns(other, right_ref, send_ref, left_ref.shape[1])
+
+
+def project_heads(arrived, value_up, left, flat_out):
     sources, block, _ = arrived.shape
     own_heads, latent_width, value_width = value_up.shape
     half = sources * block // own_heads // 2
-    feature = flat_out.shape[1]
+    depth, feature = flat_out.shape
     return pl.pallas_call(
         head_kernel,
         out_shape=[
             jax.ShapeDtypeStruct((half, feature), jnp.bfloat16),
             jax.ShapeDtypeStruct((half, own_heads * value_width), jnp.bfloat16),
-            pltpu.VMEM(gate.shape, gate.dtype),
+            pltpu.VMEM((depth, feature - left.shape[1]), flat_out.dtype),
         ],
         in_specs=[VMEM_SPEC] * 3 + [HBM_SPEC],
         out_specs=[VMEM_SPEC] * 3,
-        scratch_shapes=[
-            pltpu.VMEM((latent_width // LANES, sources * block, LANES), jnp.float32),
-            pltpu.SemaphoreType.DMA,
-        ],
+        scratch_shapes=[pltpu.SemaphoreType.DMA],
         compiler_params=pltpu.CompilerParams(vmem_limit_bytes=16 << 20),
-    )(place(arrived), place(value_up), place(flat_out), stay(gate))
-
-
-def own_kernel(heads_ref, out_ref, up_hbm, keep_ref, up_ref, sem):
-    load = pltpu.make_async_copy(up_hbm, up_ref, sem)
-    load.start()
-    step = column_step(out_ref.shape[1])
-    for k in range(out_ref.shape[1] // step):
-        columns = slice(k * step, (k + 1) * step)
-        keep_ref[:, columns] = jnp.dot(
-            heads_ref[...], out_ref[:, columns], preferred_element_type=jnp.float32
-        )
-    load.wait()
-
-
-def project_own(heads, flat_out, up):
-    rows, feature = heads.shape[0], flat_out.shape[1]
+    )(place(arrived), place(value_up), place(left), stay(flat_out))
+
+
+def own_kernel(heads_ref, left_ref, right_ref, keep_ref):
+    heads = heads_ref[...]
+    project_columns(heads, left_ref, keep_ref, 0)
+    project_columns(heads, right_ref, keep_ref, left_ref.shape[1])
+
+
+def project_own(heads, left, right):
+    rows, feature = heads.shape[0], left.shape[1] + right.shape[1]
+    size = heads.shape[1] * feature
     return pl.pallas_call(
         own_kernel,
-        out_shape=[
-            jax.ShapeDtypeStruct((rows, feature), jnp.float32),
-            pltpu.VMEM(up.shape, up.dtype),
-        ],
-        in_specs=[VMEM_SPEC] * 2 + [HBM_SPEC],
-        out_specs=[VMEM_SPEC] * 2,
-        scratch_shapes=[pltpu.SemaphoreType.DMA],
+        out_shape=jax.ShapeDtypeStruct((rows, feature), jnp.float32),
+        in_specs=[VMEM_SPEC] * 3,
+        out_specs=VMEM_SPEC,
         compiler_params=pltpu.CompilerParams(vmem_limit_bytes=4 << 20),
         cost_estimate=pl.CostEstimate(
-            flops=2 * rows * flat_out.size,
-            bytes_accessed=2 * flat_out.size + 2 * up.size,
-            transcendentals=0,
+            flops=2 * rows * size, bytes_accessed=2 * size, transcendentals=0
         ),
-    )(place(heads), place(flat_out), stay(up))
+    )(place(heads), place(left), place(right))
+
+
+def load_kernel(after_ref, gate_hbm, up_hbm, gate_ref, up_ref, sems):
+    loads = [
+        pltpu.make_async_copy(gate_hbm, gate_ref, sems.at[0]),
+        pltpu.make_async_copy(up_hbm, up_ref, sems.at[1]),
+    ]
+    for copy in loads:
+        copy.start()
+    for copy in loads:
+        copy.wait()
+
+
+def load_weights(after, gate, up):
+    return pl.pallas_call(
+        load_kernel,
+        out_shape=[pltpu.VMEM(gate.shape, gate.dtype), pltpu.VMEM(up.shape, up.dtype)],
+        in_specs=[VMEM_SPEC] + [HBM_SPEC] * 2,
+        out_specs=[VMEM_SPEC] * 2,
+        scratch_shapes=[pltpu.SemaphoreType.DMA((2,))],
+        compiler_params=pltpu.CompilerParams(vmem_limit_bytes=1 << 20),
+        cost_estimate=pl.CostEstimate(
+            flops=0, bytes_accessed=2 * (gate.size + up.size), transcendentals=0
+        ),
+    )(place(after), stay(gate), stay(up))
 
 
 def sum_kernel(zones, keep_ref, other_ref, out_ref):
@@ -357,6 +358,7 @@
     gain_ref,
     ids_ref,
     share_ref,
+    ready_ref,
     rows_ref,
     stream_ref,
     coefficient_ref,
@@ -410,7 +412,7 @@
         rows_ref[:, :, columns] = chosen.astype(jnp.bfloat16).reshape(members, zone_slots, step)
 
 
-def route(part, other, gain, expert_ids, expert_weights, experts, capacity):
+def route(part, other, gain, expert_ids, expert_weights, ready, experts, capacity):
     rows, feature = part.shape
     tokens = rows // 2
     slots = -(-experts * capacity // LANES) * LANES
@@ -421,7 +423,7 @@
             jax.ShapeDtypeStruct((tokens, feature), jnp.float32),
             jax.ShapeDtypeStruct((tokens, slots), jnp.float32),
         ],
-        in_specs=[VMEM_SPEC] * 5,
+        in_specs=[VMEM_SPEC] * 6,
         out_specs=[VMEM_SPEC] * 3,
         scratch_shapes=[pltpu.VMEM(part.shape, jnp.float32)],
         compiler_params=pltpu.CompilerParams(vmem_limit_bytes=4 << 20),
@@ -431,6 +433,7 @@
         gain.reshape(feature // LANES, LANES),
         expert_ids,
         expert_weights,
+        place(ready),
     )
 
 
@@ -470,7 +473,7 @@
 
 def fill_hidden(rows, gate_ref, up_ref, hidden_ref):
     width = gate_ref.shape[1]
-    step = 256 if width % 256 == 0 else width
+    step = 512 if width % 512 == 0 else width
     for k in range(width // step):
         columns = slice(k * step, (k + 1) * step)
         gate_part = jnp.dot(rows, gate_ref[:, columns], preferred_element_type=jnp.float32)
@@ -480,17 +483,20 @@
         )
 
 
-def fill_partial(hidden, down_ref, out_ref):
-    step = column_step(down_ref.shape[1])
-    for k in range(down_ref.shape[1] // step):
+def fill_partial(hidden, top_ref, bottom_ref, out_ref):
+    depth, feature = top_ref.shape
+    step = column_step(feature)
+    for k in range(feature // step):
         columns = slice(k * step, (k + 1) * step)
-        out_ref[:, columns] = jnp.dot(
-            hidden, down_ref[:, columns], preferred_element_type=jnp.float32
-        ).astype(jnp.bfloat16)
-
-
-def own_hidden_kernel(rows_ref, gate_ref, up_ref, down_hbm, hidden_ref, down_ref, sem):
-    load = pltpu.make_async_copy(down_hbm, down_ref, sem)
+        out = jnp.dot(hidden[:, :depth], top_ref[:, columns], preferred_element_type=jnp.float32)
+        out = out + jnp.dot(
+            hidden[:, depth:], bottom_ref[:, columns], preferred_element_type=jnp.float32
+        )
+        out_ref[:, columns] = out.astype(jnp.bfloat16)
+
+
+def own_hidden_kernel(rows_ref, gate_ref, up_ref, down_hbm, hidden_ref, top_ref, sem):
+    load = pltpu.make_async_copy(down_hbm.at[pl.ds(0, top_ref.shape[0])], top_ref, sem)
     load.start()
     shape = rows_ref.shape
     rows = rows_ref[...].reshape(shape[0] * shape[1], shape[2])
@@ -504,52 +510,65 @@
         own_hidden_kernel,
         out_shape=[
             jax.ShapeDtypeStruct((count, gate.shape[1]), jnp.bfloat16),
-            pltpu.VMEM(down.shape, down.dtype),
+            pltpu.VMEM((down.shape[0] // 2, down.shape[1]), down.dtype),
         ],
         in_specs=[VMEM_SPEC] * 3 + [HBM_SPEC],
         out_specs=[VMEM_SPEC] * 2,
         scratch_shapes=[pltpu.SemaphoreType.DMA],
         compiler_params=pltpu.CompilerParams(vmem_limit_bytes=8 << 20),
         cost_estimate=pl.CostEstimate(
-            flops=4 * count * gate.size, bytes_accessed=6 * gate.size, transcendentals=0
+            flops=4 * count * gate.size, bytes_accessed=5 * gate.size, transcendentals=0
         ),
     )(place(rows), place(gate), place(up), stay(down))
 
 
-def other_partial_kernel(rows_ref, gate_ref, up_ref, down_ref, send_ref, hidden_ref):
+def other_partial_kernel(
+    rows_ref, gate_ref, up_ref, top_ref, down_hbm, send_ref, bottom_ref, hidden_ref, sem
+):
+    depth = bottom_ref.shape[0]
+    load = pltpu.make_async_copy(down_hbm.at[pl.ds(depth, depth)], bottom_ref, sem)
+    load.start()
     shape = rows_ref.shape
     rows = rows_ref[...].reshape(shape[0] * shape[1], shape[2])
     fill_hidden(rows, gate_ref, up_ref, hidden_ref)
-    fill_partial(hidden_ref[...], down_ref, send_ref)
-
-
-def other_partial(rows, gate, up, down):
+    load.wait()
+    fill_partial(hidden_ref[...], top_ref, bottom_ref, send_ref)
+
+
+def other_partial(rows, gate, up, top, down):
     count, feature = rows.shape[0] * rows.shape[1], rows.shape[2]
     return pl.pallas_call(
         other_partial_kernel,
-        out_shape=jax.ShapeDtypeStruct((count, feature), jnp.bfloat16),
-        in_specs=[VMEM_SPEC] * 4,
-        out_specs=VMEM_SPEC,
-        scratch_shapes=[pltpu.VMEM((count, gate.shape[1]), jnp.bfloat16)],
+        out_shape=[
+            jax.ShapeDtypeStruct((count, feature), jnp.bfloat16),
+            pltpu.VMEM(top.shape, top.dtype),
+        ],
+        in_specs=[VMEM_SPEC] * 4 + [HBM_SPEC],
+        out_specs=[VMEM_SPEC] * 2,
+        scratch_shapes=[
+            pltpu.VMEM((count, gate.shape[1]), jnp.bfloat16),
+            pltpu.SemaphoreType.DMA,
+        ],
         compiler_params=pltpu.CompilerParams(vmem_limit_bytes=8 << 20),
-    )(place(rows), place(gate), place(up), place(down))
-
-
-def own_partial_kernel(hidden_ref, down_ref, keep_ref):
-    fill_partial(hidden_ref[...], down_ref, keep_ref)
-
-
-def own_partial(hidden, down):
+    )(place(rows), place(gate), place(up), place(top), stay(down))
+
+
+def own_partial_kernel(hidden_ref, top_ref, bottom_ref, keep_ref):
+    fill_partial(hidden_ref[...], top_ref, bottom_ref, keep_ref)
+
+
+def own_partial(hidden, top, bottom):
+    rows, feature = hidden.shape[0], top.shape[1]
     return pl.pallas_call(
         own_partial_kernel,
-        out_shape=jax.ShapeDtypeStruct((hidden.shape[0], down.shape[1]), jnp.bfloat16),
-        in_specs=[VMEM_SPEC] * 2,
+        out_shape=jax.ShapeDtypeStruct((rows, feature), jnp.bfloat16),
+        in_specs=[VMEM_SPEC] * 3,
         out_specs=VMEM_SPEC,
         compiler_params=pltpu.CompilerParams(vmem_limit_bytes=4 << 20),
         cost_estimate=pl.CostEstimate(
-            flops=2 * hidden.shape[0] * down.size, bytes_accessed=2 * down.size, transcendentals=0
+            flops=4 * rows * top.size, bytes_accessed=4 * top.size, transcendentals=0
         ),
-    )(place(hidden), place(down))
+    )(place(hidden), place(top), place(bottom))
 
 
 def swap_sides(block):
@@ -581,13 +600,13 @@
         row_count, max(2, (row_count * expert_ids.shape[1] + ep_count - 1) // ep_count)
     )
 
-    latent, value_up, flat_out = attend(
+    latent, value_up, left = attend(
         queries, latent_cache, new_latent, lengths, value_up, flat_out, ep_count * side_count
     )
     arrived = lax.all_to_all(latent, ("ep", "side"), split_axis=0, concat_axis=0, tiled=True)
-    send, own_heads, gate = project_heads(arrived, value_up, flat_out, gate_proj[0])
+    send, own_heads, right = project_heads(arrived, value_up, left, flat_out)
     from_other = swap_sides(send)
-    keep, up = project_own(own_heads, flat_out, up_proj[0])
+    keep = project_own(own_heads, left, right)
     members = ep_count // 2
     zones = [list(range(members)), list(range(members, ep_count))]
     contribution = sum_halves(keep, from_other, members, 1)
@@ -598,17 +617,18 @@
     other_part = lax.ppermute(
         part_copy, "ep", [(e, (e + members) % ep_count) for e in range(ep_count)]
     )
+    gate, up = load_weights(part_copy, gate_proj[0], up_proj[0])
     outbound, stream, coefficient = route(
-        part, other_part, norm_gain, expert_ids, expert_weights, ep_count, capacity
+        part, other_part, norm_gain, expert_ids, expert_weights, gate, ep_count, capacity
     )
     own_rows = lax.all_to_all(
         outbound, "ep", split_axis=0, concat_axis=0, tiled=True, axis_index_groups=zones
     )
     other_rows = swap_sides(own_rows)
-    hidden, down = own_hidden(own_rows, gate, up, down_proj[0])
-    send = other_partial(other_rows, gate, up, down)
+    hidden, top = own_hidden(own_rows, gate, up, down_proj[0])
+    send, bottom = other_partial(other_rows, gate, up, top, down_proj[0])
     other = swap_sides(send)
-    keep = own_partial(hidden, down)
+    keep = own_partial(hidden, top, bottom)
     both = sum_halves(keep, other, ep_count, 2)
     returned = lax.all_to_all(both, "ep", split_axis=0, concat_axis=0, tiled=True)
     return mix(returned, coefficient, stream)

time: 77.1 us -> 75.4 us (0.978)
  waiting for transfers between devices: 4.72 us -> 2.54 us
  Pallas kernels: 13.2 us -> 14.1 us
    ppermute x1, waiting for transfers between devices: 4.32 us -> 1.11 us  [local(): lax.ppermute(part_copy, 'ep', [(e, (e + members) % ep_count) for e in ran...]
    pallas_call x3 -> x4, Pallas kernels: 4.81 us -> 6.92 us  [the longest x1 3.19 us: load_weights(): pl.pallas_call(load_kernel, out_shape=[pltpu.VMEM(gate.shape, gate.dtype)...]
    ppermute x3, waiting for transfers between devices: 0.4 us -> 1.43 us  [swap_sides(): return lax.ppermute(block, 'side', [(0, 1), (1, 0)])]
  transfers between devices with their start and end apart: 4 -> 4, of which waited for: 2 -> 3; matrix products, arithmetic and copies ran while one was open for 0% -> 0% of each run, Pallas kernels for 6% -> 8%
where the time goes in v4:
time: 75.4 us; the launch traced here: 75.1 us
  blocking collectives  56.2 us (75%)
  Pallas kernels  14.1 us (19%)
  waiting for transfers between devices  2.54 us (3%)
  starting transfers between devices  2.13 us (3%)
    all_to_all x1, blocking collectives, local(): lax.all_to_all(latent, ('ep', 'side'), split_axis=0, concat_axis=0, tiled...  22.7 us
    all_to_all x1, blocking collectives, local(): lax.all_to_all(both, 'ep', split_axis=0, concat_axis=0, tiled=True)  12.6 us
    all_to_all x1, blocking collectives, local(): lax.all_to_all(contribution, 'ep', split_axis=0, concat_axis=0, tiled=Tru...  11.9 us
    all_to_all x1, blocking collectives, local(): lax.all_to_all(outbound, 'ep', split_axis=0, concat_axis=0, tiled=True, a...  8.9 us
    pallas_call x1, Pallas kernels, load_weights(): pl.pallas_call(load_kernel, out_shape=[pltpu.VMEM(gate.shape, gate.dtype)...  3.19 us
    pallas_call x1, Pallas kernels, attend(): pl.pallas_call(attention_kernel, out_shape=[jax.ShapeDtypeStruct((holders...  2.54 us
    pallas_call x1, Pallas kernels, other_partial(): pl.pallas_call(other_partial_kernel, out_shape=[jax.ShapeDtypeStruct((cou...  2.26 us
    pallas_call x1, Pallas kernels, project_heads(): pl.pallas_call(head_kernel, out_shape=[jax.ShapeDtypeStruct((half, featur...  1.67 us
  transfers between devices with their start and end apart: 4, of which 3 were waited for; matrix products, arithmetic and copies ran while one was open for 0% of the time, Pallas kernels for 8%

profile of v4, /device:TPU:0, one launch (start us, length us, event | category | flops | bytes accessed | tf_op | source)
XLA Modules:
  0.0 75.1 jit_solution(17382321349885829593)
XLA Ops:
  0.0 2.5 %shard_map.127 = (bf16[32,16,512]{2,1,0:T(8,128)(2,1)S(1)}, bf16[4,512,128]{2,1,0:T(8,128)(2,1)S(1)}, bf16[512,2560]{1,0:T(8,128)(2,1)S(1)}) custom-call(s32[2]{0:T(128)} %lengths_hbm.1, bf16[4,576,128]{2,1,0:T(8,128)(2,1)} %bitcast.14, bf16[2,576,128]{2,1,0:T(8,128)(2,1)} %bitcast.15, bf16[4,576]{1,0:T(4,128)(2,1)} %fresh_hbm.1, ...), custom_call_target="tpu_custom_call" | custom-call | tf_op jit(solution)/shard_map/pallas_call | solution.py:153
  2.6 22.7 %all_to_all.20.arrived_ref = bf16[32,16,512]{2,1,0:T(8,128)(2,1)S(1)} all-to-all(bf16[32,16,512]{2,1,0:T(8,128)(2,1)S(1)} %get-tuple-element.22), channel_id=1, replica_groups=mesh['groups'=1,'ep'=16,'side'=2] {'ep','side'}, dimensions={0} | all-to-all | bytes 1048576 | tf_op jit(solution)/shard_map/all_to_all | solution.py:606
  25.3 1.7 %shard_map.128 = (bf16[64,3584]{1,0:T(8,128)(2,1)S(1)}, bf16[64,512]{1,0:T(8,128)(2,1)S(1)}, bf16[512,1024]{1,0:T(8,128)(2,1)S(1)}) custom-call(bf16[32,16,512]{2,1,0:T(8,128)(2,1)S(1)} %all_to_all.20.arrived_ref, bf16[4,512,128]{2,1,0:T(8,128)(2,1)S(1)} %get-tuple-element.23.up_ref, bf16[512,2560]{1,0:T(8,128)(2,1)S(1)} %get-tuple-element.24.left_ref, ...), custom_call_target="tpu_custom_call" | custom-call | tf_op jit(solution)/shard_map/pallas_call | solution.py:217
  27.0 0.1 collective-permute-start
  27.1 0.0 copy-start
  27.1 0.0 copy-start.2
  27.1 0.7 shard_map.129.keep_ref
  27.8 1.0 %collective-permute-done.other_ref = bf16[64,3584]{1,0:T(8,128)(2,1)S(1)} collective-permute-done((bf16[64,3584]{1,0:T(8,128)(2,1)S(1)}, bf16[64,3584]{1,0:T(8,128)(2,1)S(1)}, u32[]{:S(2)}, u32[]{:S(2)}) %collective-permute-start) | collective-permute-done | bytes 458784 | tf_op jit(solution)/shard_map/ppermute | solution.py:575
  28.9 0.1 shard_map.130
  28.9 11.9 %all_to_all.21.shared_ref = bf16[8,8,3584]{2,1,0:T(8,128)(2,1)S(1)} all-to-all(bf16[8,8,3584]{2,1,0:T(8,128)(2,1)S(1)} %shard_map.130), channel_id=1, replica_groups={{0,2,4,6,8,10,12,14},{16,18,20,22,24,26,28,30},{1,3,5,7,9,11,13,15},{17..., dimensions={0} | all-to-all | bytes 917504 | tf_op jit(solution)/shard_map/all_to_all | solution.py:613
  40.9 0.0 copy-done
  40.9 0.0 copy-done.2
  40.9 0.1 shard_map.131
  41.0 1.5 %collective-permute-start.1 = (bf16[8,3712]{1,0:T(8,128)(2,1)S(1)}, bf16[8,3712]{1,0:T(8,128)(2,1)S(1)}, u32[]{:S(2)}, u32[]{:S(2)}) collective-permute-start(bf16[8,3712]{1,0:T(8,128)(2,1)S(1)} %get-tuple-element.29.after_ref), channel_id=1, source_target_pairs={{0,16},{2,18},{4,20},{6,22},{8,24},{10,26},{12,28},{14,30},{16,0},... | collective-permute-start | bytes 178184 | tf_op jit(solution)/shard_map/ppermute | solution.py:617
  42.4 0.0 copy-start.1
  42.5 0.0 copy-start.3
  42.5 3.2 %shard_map.132 = (bf16[3584,512]{1,0:T(8,128)(2,1)S(1)}, bf16[3584,512]{1,0:T(8,128)(2,1)S(1)}) custom-call(bf16[8,3712]{1,0:T(8,128)(2,1)S(1)} %get-tuple-element.29.after_ref, bf16[3584,512]{1,0:T(8,128)(2,1)} %bitcast.12, bf16[3584,512]{1,0:T(8,128)(2,1)} %bitcast.13), custom_call_target="tpu_custom_call" | custom-call | bytes 7340032 | tf_op jit(solution)/shard_map/pallas_call | solution.py:264
  45.7 1.1 %collective-permute-done.1.other_ref = bf16[8,3712]{1,0:T(8,128)(2,1)S(1)} collective-permute-done((bf16[8,3712]{1,0:T(8,128)(2,1)S(1)}, bf16[8,3712]{1,0:T(8,128)(2,1)S(1)}, u32[]{:S(2)}, u32[]{:S(2)}) %collective-permute-start.1) | collective-permute-done | bytes 59424 | tf_op jit(solution)/shard_map/ppermute | solution.py:617
  46.8 0.0 copy-done.1
  46.8 0.0 copy-done.3
  46.8 0.4 shard_map.133
  47.1 8.9 %all_to_all.22.rows_ref = bf16[8,4,3584]{2,1,0:T(4,128)(2,1)S(1)} all-to-all(bf16[8,4,3584]{2,1,0:T(4,128)(2,1)S(1)} %get-tuple-element.31), channel_id=1, replica_groups={{0,2,4,6,8,10,12,14},{16,18,20,22,24,26,28,30},{1,3,5,7,9,11,13,15},{17..., dimensions={0} | all-to-all | bytes 458752 | tf_op jit(solution)/shard_map/all_to_all | solution.py:624
  56.0 0.0 collective-permute-start.2
  56.0 1.5 %shard_map.134 = (bf16[32,512]{1,0:T(8,128)(2,1)S(1)}, bf16[256,3584]{1,0:T(8,128)(2,1)S(1)}) custom-call(bf16[8,4,3584]{2,1,0:T(4,128)(2,1)S(1)} %all_to_all.22.rows_ref, bf16[3584,512]{1,0:T(8,128)(2,1)S(1)} %get-tuple-element.30.ready_ref.gate_ref, bf16[3584,512]{1,0:T(8,128)(2,1)S(1)} %get-tuple-element.32.up_ref, bf16[512,3584]{1,0:T(8,128)(2,1)} %bitcast.10), custom_call_target="tpu_custom_call" | custom-call | flops 234881024 | bytes 9175040 | tf_op jit(solution)/shard_map/pallas_call | solution.py:509
  57.6 0.0 collective-permute-done.2.rows_ref
  57.6 2.3 %shard_map.135 = (bf16[32,3584]{1,0:T(8,128)(2,1)S(1)}, bf16[256,3584]{1,0:T(8,128)(2,1)S(1)}) custom-call(bf16[8,4,3584]{2,1,0:T(4,128)(2,1)S(1)} %collective-permute-done.2.rows_ref, bf16[3584,512]{1,0:T(8,128)(2,1)S(1)} %get-tuple-element.30.ready_ref.gate_ref, bf16[3584,512]{1,0:T(8,128)(2,1)S(1)} %get-tuple-element.32.up_ref, ...), custom_call_target="tpu_custom_call" | custom-call | tf_op jit(solution)/shard_map/pallas_call | solution.py:540
  59.9 0.6 collective-permute-start.3
  60.4 0.7 shard_map.136.keep_ref
  61.1 0.4 collective-permute-done.3.other_ref
  61.5 0.1 shard_map.137
  61.6 12.6 %all_to_all.23.returned_ref = bf16[16,2,3584]{2,1,0:T(2,128)(2,1)S(1)} all-to-all(bf16[16,2,3584]{2,1,0:T(2,128)(2,1)S(1)} %shard_map.137), channel_id=1, replica_groups=mesh['groups'=1,'ep'=16,'side'=2] {'ep'}, dimensions={0} | all-to-all | bytes 458752 | tf_op jit(solution)/shard_map/all_to_all | solution.py:633
  74.3 0.8 %shard_map.138 = bf16[4,3584]{1,0:T(4,128)(2,1)} custom-call(bf16[16,2,3584]{2,1,0:T(2,128)(2,1)S(1)} %all_to_all.23.returned_ref, f32[4,128]{1,0:T(4,128)S(1)} %get-tuple-element.37.coefficient_ref, f32[4,3584]{1,0:T(4,128)S(1)} %get-tuple-element.38.stream_ref), custom_call_target="tpu_custom_call" | custom-call | tf_op jit(solution)/shard_map/pallas_call | solution.py:465
Async XLA Ops:
  27.0 1.9 %collective-permute-start = (bf16[64,3584]{1,0:T(8,128)(2,1)S(1)}, bf16[64,3584]{1,0:T(8,128)(2,1)S(1)}, u32[]{:S(2)}, u32[]{:S(2)}) collective-permute-start(bf16[64,3584]{1,0:T(8,128)(2,1)S(1)} %get-tuple-element.27), channel_id=1, source_target_pairs={{0,1},{1,0},{2,3},{3,2},{4,5},{5,4},{6,7},{7,6},{8,9},{9,8},{10,11... | collective-permute-start | bytes 1376264 | tf_op jit(solution)/shard_map/ppermute | solution.py:575
  27.1 13.8 %copy-start = (bf16[4,3584]{1,0:T(4,128)(2,1)S(1)}, bf16[4,3584]{1,0:T(4,128)(2,1)}, u32[]{:S(2)}) copy-start(bf16[4,3584]{1,0:T(4,128)(2,1)} %residual_ref.1) | copy-start | bytes 86020
  27.1 13.8 %copy-start.2 = (s32[4,8]{1,0:T(4,128)S(1)}, s32[4,8]{1,0:T(4,128)}, u32[]{:S(2)}) copy-start(s32[4,8]{1,0:T(4,128)} %ids_ref.3) | copy-start | bytes 388
  41.0 5.8 %collective-permute-start.1 = (bf16[8,3712]{1,0:T(8,128)(2,1)S(1)}, bf16[8,3712]{1,0:T(8,128)(2,1)S(1)}, u32[]{:S(2)}, u32[]{:S(2)}) collective-permute-start(bf16[8,3712]{1,0:T(8,128)(2,1)S(1)} %get-tuple-element.29.after_ref), channel_id=1, source_target_pairs={{0,16},{2,18},{4,20},{6,22},{8,24},{10,26},{12,28},{14,30},{16,0},... | collective-permute-start | bytes 178184 | tf_op jit(solution)/shard_map/ppermute | solution.py:617
  42.4 4.3 %copy-start.1 = (f32[3584]{0:T(1024)S(1)}, f32[3584]{0:T(1024)}, u32[]{:S(2)}) copy-start(f32[3584]{0:T(1024)} %param.18) | copy-start | bytes 43012
  42.5 4.3 %copy-start.3 = (f32[4,8]{1,0:T(4,128)S(1)}, f32[4,8]{1,0:T(4,128)}, u32[]{:S(2)}) copy-start(f32[4,8]{1,0:T(4,128)} %share_ref.1) | copy-start | bytes 388
  56.0 1.5 %collective-permute-start.2 = (bf16[8,4,3584]{2,1,0:T(4,128)(2,1)S(1)}, bf16[8,4,3584]{2,1,0:T(4,128)(2,1)S(1)}, u32[]{:S(2)}, u32[]{:S(2)}) collective-permute-start(bf16[8,4,3584]{2,1,0:T(4,128)(2,1)S(1)} %all_to_all.22.rows_ref), channel_id=1, source_target_pairs={{0,1},{1,0},{2,3},{3,2},{4,5},{5,4},{6,7},{7,6},{8,9},{9,8},{10,11... | collective-permute-start | bytes 688136 | tf_op jit(solution)/shard_map/ppermute | solution.py:575
  59.9 1.7 %collective-permute-start.3 = (bf16[32,3584]{1,0:T(8,128)(2,1)S(1)}, bf16[32,3584]{1,0:T(8,128)(2,1)S(1)}, u32[]{:S(2)}, u32[]{:S(2)}) collective-permute-start(bf16[32,3584]{1,0:T(8,128)(2,1)S(1)} %get-tuple-element.36), channel_id=1, source_target_pairs={{0,1},{1,0},{2,3},{3,2},{4,5},{5,4},{6,7},{7,6},{8,9},{9,8},{10,11... | collective-permute-start | bytes 688136 | tf_op jit(solution)/shard_map/ppermute | solution.py:575

commit v5 on v4

--- a/solution.py
+++ b/solution.py
@@ -122,7 +122,7 @@
         live = (row < lengths_ref[r]) | fresh_live
         scores = jnp.where(live, scores, masked_score)
         highest = jnp.max(scores, axis=0, keepdims=True)
-        weights = jnp.where(live, jnp.exp(scores - highest), 0.0)
+        weights = jnp.exp(scores - highest)
         inverse = 1.0 / jnp.sum(weights, axis=0, keepdims=True)
         tail = weights[context:]
         for n in range(3):
@@ -249,10 +249,11 @@
     )(place(heads), place(left), place(right))
 
 
-def load_kernel(after_ref, gate_hbm, up_hbm, gate_ref, up_ref, sems):
+def load_kernel(after_ref, gate_hbm, up_hbm, down_hbm, gate_ref, up_ref, top_ref, sems):
     loads = [
         pltpu.make_async_copy(gate_hbm, gate_ref, sems.at[0]),
         pltpu.make_async_copy(up_hbm, up_ref, sems.at[1]),
+        pltpu.make_async_copy(down_hbm.at[pl.ds(0, top_ref.shape[0])], top_ref, sems.at[2]),
     ]
     for copy in loads:
         copy.start()
@@ -260,18 +261,19 @@
         copy.wait()
 
 
-def load_weights(after, gate, up):
+def load_weights(after, gate, up, down):
+    top = pltpu.VMEM((down.shape[0] // 2, down.shape[1]), down.dtype)
     return pl.pallas_call(
         load_kernel,
-        out_shape=[pltpu.VMEM(gate.shape, gate.dtype), pltpu.VMEM(up.shape, up.dtype)],
-        in_specs=[VMEM_SPEC] + [HBM_SPEC] * 2,
-        out_specs=[VMEM_SPEC] * 2,
-        scratch_shapes=[pltpu.SemaphoreType.DMA((2,))],
+        out_shape=[pltpu.VMEM(gate.shape, gate.dtype), pltpu.VMEM(up.shape, up.dtype), top],
+        in_specs=[VMEM_SPEC] + [HBM_SPEC] * 3,
+        out_specs=[VMEM_SPEC] * 3,
+        scratch_shapes=[pltpu.SemaphoreType.DMA((3,))],
         compiler_params=pltpu.CompilerParams(vmem_limit_bytes=1 << 20),
         cost_estimate=pl.CostEstimate(
-            flops=0, bytes_accessed=2 * (gate.size + up.size), transcendentals=0
+            flops=0, bytes_accessed=2 * (gate.size + up.size + down.size // 2), transcendentals=0
         ),
-    )(place(after), stay(gate), stay(up))
+    )(place(after), stay(gate), stay(up), stay(down))
 
 
 def sum_kernel(zones, keep_ref, other_ref, out_ref):
@@ -495,8 +497,11 @@
         out_ref[:, columns] = out.astype(jnp.bfloat16)
 
 
-def own_hidden_kernel(rows_ref, gate_ref, up_ref, down_hbm, hidden_ref, top_ref, sem):
-    load = pltpu.make_async_copy(down_hbm.at[pl.ds(0, top_ref.shape[0])], top_ref, sem)
+def own_hidden_kernel(rows_ref, gate_ref, up_ref, down_hbm, hidden_ref, bottom_ref, sem):
+    depth = bottom_ref.shape[0]
+    load = pltpu.make_async_copy(
+        down_hbm.at[pl.ds(down_hbm.shape[0] - depth, depth)], bottom_ref, sem
+    )
     load.start()
     shape = rows_ref.shape
     rows = rows_ref[...].reshape(shape[0] * shape[1], shape[2])
@@ -504,13 +509,13 @@
     load.wait()
 
 
-def own_hidden(rows, gate, up, down):
+def own_hidden(rows, gate, up, down, top):
     count = rows.shape[0] * rows.shape[1]
     return pl.pallas_call(
         own_hidden_kernel,
         out_shape=[
             jax.ShapeDtypeStruct((count, gate.shape[1]), jnp.bfloat16),
-            pltpu.VMEM((down.shape[0] // 2, down.shape[1]), down.dtype),
+            pltpu.VMEM((down.shape[0] - top.shape[0], down.shape[1]), down.dtype),
         ],
         in_specs=[VMEM_SPEC] * 3 + [HBM_SPEC],
         out_specs=[VMEM_SPEC] * 2,
@@ -522,35 +527,23 @@
     )(place(rows), place(gate), place(up), stay(down))
 
 
-def other_partial_kernel(
-    rows_ref, gate_ref, up_ref, top_ref, down_hbm, send_ref, bottom_ref, hidden_ref, sem
-):
-    depth = bottom_ref.shape[0]
-    load = pltpu.make_async_copy(down_hbm.at[pl.ds(depth, depth)], bottom_ref, sem)
-    load.start()
+def other_partial_kernel(rows_ref, gate_ref, up_ref, top_ref, bottom_ref, send_ref, hidden_ref):
     shape = rows_ref.shape
     rows = rows_ref[...].reshape(shape[0] * shape[1], shape[2])
     fill_hidden(rows, gate_ref, up_ref, hidden_ref)
-    load.wait()
     fill_partial(hidden_ref[...], top_ref, bottom_ref, send_ref)
 
 
-def other_partial(rows, gate, up, top, down):
+def other_partial(rows, gate, up, top, bottom):
     count, feature = rows.shape[0] * rows.shape[1], rows.shape[2]
     return pl.pallas_call(
         other_partial_kernel,
-        out_shape=[
-            jax.ShapeDtypeStruct((count, feature), jnp.bfloat16),
-            pltpu.VMEM(top.shape, top.dtype),
-        ],
-        in_specs=[VMEM_SPEC] * 4 + [HBM_SPEC],
-        out_specs=[VMEM_SPEC] * 2,
-        scratch_shapes=[
-            pltpu.VMEM((count, gate.shape[1]), jnp.bfloat16),
-            pltpu.SemaphoreType.DMA,
-        ],
+        out_shape=jax.ShapeDtypeStruct((count, feature), jnp.bfloat16),
+        in_specs=[VMEM_SPEC] * 5,
+        out_specs=VMEM_SPEC,
+        scratch_shapes=[pltpu.VMEM((count, gate.shape[1]), jnp.bfloat16)],
         compiler_params=pltpu.CompilerParams(vmem_limit_bytes=8 << 20),
-    )(place(rows), place(gate), place(up), place(top), stay(down))
+    )(place(rows), place(gate), place(up), place(top), place(bottom))
 
 
 def own_partial_kernel(hidden_ref, top_ref, bottom_ref, keep_ref):
@@ -617,7 +610,7 @@
     other_part = lax.ppermute(
         part_copy, "ep", [(e, (e + members) % ep_count) for e in range(ep_count)]
     )
-    gate, up = load_weights(part_copy, gate_proj[0], up_proj[0])
+    gate, up, top = load_weights(part_copy, gate_proj[0], up_proj[0], down_proj[0])
     outbound, stream, coefficient = route(
         part, other_part, norm_gain, expert_ids, expert_weights, gate, ep_count, capacity
     )
@@ -625,8 +618,8 @@
         outbound, "ep", split_axis=0, concat_axis=0, tiled=True, axis_index_groups=zones
     )
     other_rows = swap_sides(own_rows)
-    hidden, top = own_hidden(own_rows, gate, up, down_proj[0])
-    send, bottom = other_partial(other_rows, gate, up, top, down_proj[0])
+    hidden, bottom = own_hidden(own_rows, gate, up, down_proj[0], top)
+    send = other_partial(other_rows, gate, up, top, bottom)
     other = swap_sides(send)
     keep = own_partial(hidden, top, bottom)
     both = sum_halves(keep, other, ep_count, 2)

time: 75.4 us -> 75.1 us (level)
  transfers between devices with their start and end apart: 4 -> 4, of which waited for: 3 -> 3; matrix products, arithmetic and copies ran while one was open for 0% -> 0% of each run, Pallas kernels for 8% -> 9%
where the time goes in v5:
time: 75.1 us; the launch traced here: 74.8 us
  blocking collectives  56.2 us (75%)
  Pallas kernels  14.3 us (19%)
  starting transfers between devices  2.09 us (3%)
  waiting for transfers between devices  2.03 us (3%)
    all_to_all x1, blocking collectives, local(): lax.all_to_all(latent, ('ep', 'side'), split_axis=0, concat_axis=0, tiled...  22.7 us
    all_to_all x1, blocking collectives, local(): lax.all_to_all(both, 'ep', split_axis=0, concat_axis=0, tiled=True)  12.6 us
    all_to_all x1, blocking collectives, local(): lax.all_to_all(contribution, 'ep', split_axis=0, concat_axis=0, tiled=Tru...  11.9 us
    all_to_all x1, blocking collectives, local(): lax.all_to_all(outbound, 'ep', split_axis=0, concat_axis=0, tiled=True, a...  8.9 us
    pallas_call x1, Pallas kernels, load_weights(): pl.pallas_call(load_kernel, out_shape=[pltpu.VMEM(gate.shape, gate.dtype)...  3.7 us
    pallas_call x1, Pallas kernels, attend(): pl.pallas_call(attention_kernel, out_shape=[jax.ShapeDtypeStruct((holders...  2.54 us
    pallas_call x1, Pallas kernels, other_partial(): pl.pallas_call(other_partial_kernel, out_shape=jax.ShapeDtypeStruct((coun...  2.04 us
    pallas_call x1, Pallas kernels, project_heads(): pl.pallas_call(head_kernel, out_shape=[jax.ShapeDtypeStruct((half, featur...  1.67 us
  transfers between devices with their start and end apart: 4, of which 3 were waited for; matrix products, arithmetic and copies ran while one was open for 0% of the time, Pallas kernels for 9%

profile of v5, /device:TPU:0, one launch (start us, length us, event | category | flops | bytes accessed | tf_op | source)
XLA Modules:
  0.0 74.8 jit_solution(8924626460343743321)
XLA Ops:
  0.0 2.5 %shard_map.127 = (bf16[32,16,512]{2,1,0:T(8,128)(2,1)S(1)}, bf16[4,512,128]{2,1,0:T(8,128)(2,1)S(1)}, bf16[512,2560]{1,0:T(8,128)(2,1)S(1)}) custom-call(s32[2]{0:T(128)} %lengths_hbm.1, bf16[4,576,128]{2,1,0:T(8,128)(2,1)} %bitcast.14, bf16[2,576,128]{2,1,0:T(8,128)(2,1)} %bitcast.15, bf16[4,576]{1,0:T(4,128)(2,1)} %fresh_hbm.1, ...), custom_call_target="tpu_custom_call" | custom-call | tf_op jit(solution)/shard_map/pallas_call | solution.py:153
  2.5 22.7 %all_to_all.20.arrived_ref = bf16[32,16,512]{2,1,0:T(8,128)(2,1)S(1)} all-to-all(bf16[32,16,512]{2,1,0:T(8,128)(2,1)S(1)} %get-tuple-element.21), channel_id=1, replica_groups=mesh['groups'=1,'ep'=16,'side'=2] {'ep','side'}, dimensions={0} | all-to-all | bytes 1048576 | tf_op jit(solution)/shard_map/all_to_all | solution.py:599
  25.3 1.7 %shard_map.128 = (bf16[64,3584]{1,0:T(8,128)(2,1)S(1)}, bf16[64,512]{1,0:T(8,128)(2,1)S(1)}, bf16[512,1024]{1,0:T(8,128)(2,1)S(1)}) custom-call(bf16[32,16,512]{2,1,0:T(8,128)(2,1)S(1)} %all_to_all.20.arrived_ref, bf16[4,512,128]{2,1,0:T(8,128)(2,1)S(1)} %get-tuple-element.22.up_ref, bf16[512,2560]{1,0:T(8,128)(2,1)S(1)} %get-tuple-element.23.left_ref, ...), custom_call_target="tpu_custom_call" | custom-call | tf_op jit(solution)/shard_map/pallas_call | solution.py:217
  27.0 0.1 collective-permute-start
  27.1 0.0 copy-start
  27.1 0.0 copy-start.2
  27.1 0.7 shard_map.129.keep_ref
  27.8 1.0 %collective-permute-done.other_ref = bf16[64,3584]{1,0:T(8,128)(2,1)S(1)} collective-permute-done((bf16[64,3584]{1,0:T(8,128)(2,1)S(1)}, bf16[64,3584]{1,0:T(8,128)(2,1)S(1)}, u32[]{:S(2)}, u32[]{:S(2)}) %collective-permute-start) | collective-permute-done | bytes 458784 | tf_op jit(solution)/shard_map/ppermute | solution.py:568
  28.9 0.1 shard_map.130
  28.9 11.9 %all_to_all.21.shared_ref = bf16[8,8,3584]{2,1,0:T(8,128)(2,1)S(1)} all-to-all(bf16[8,8,3584]{2,1,0:T(8,128)(2,1)S(1)} %shard_map.130), channel_id=1, replica_groups={{0,2,4,6,8,10,12,14},{16,18,20,22,24,26,28,30},{1,3,5,7,9,11,13,15},{17..., dimensions={0} | all-to-all | bytes 917504 | tf_op jit(solution)/shard_map/all_to_all | solution.py:606
  40.9 0.0 copy-done
  40.9 0.0 copy-done.2
  40.9 0.1 shard_map.131
  41.0 1.5 %collective-permute-start.1 = (bf16[8,3712]{1,0:T(8,128)(2,1)S(1)}, bf16[8,3712]{1,0:T(8,128)(2,1)S(1)}, u32[]{:S(2)}, u32[]{:S(2)}) collective-permute-start(bf16[8,3712]{1,0:T(8,128)(2,1)S(1)} %get-tuple-element.28.after_ref), channel_id=1, source_target_pairs={{0,16},{2,18},{4,20},{6,22},{8,24},{10,26},{12,28},{14,30},{16,0},... | collective-permute-start | bytes 178184 | tf_op jit(solution)/shard_map/ppermute | solution.py:610
  42.4 0.0 copy-start.1
  42.4 0.0 copy-start.3
  42.5 3.7 %shard_map.132 = (bf16[3584,512]{1,0:T(8,128)(2,1)S(1)}, bf16[3584,512]{1,0:T(8,128)(2,1)S(1)}, bf16[256,3584]{1,0:T(8,128)(2,1)S(1)}) custom-call(bf16[8,3712]{1,0:T(8,128)(2,1)S(1)} %get-tuple-element.28.after_ref, bf16[3584,512]{1,0:T(8,128)(2,1)} %bitcast.12, bf16[3584,512]{1,0:T(8,128)(2,1)} %bitcast.13, bf16[512,3584]{1,0:T(8,128)(2,1)} %bitcast.10), custom_call_target="tpu_custom_call" | custom-call | bytes 9175040 | tf_op jit(solution)/shard_map/pallas_call | solution.py:266
  46.2 0.6 collective-permute-done.1.other_ref
  46.8 0.0 copy-done.1
  46.8 0.0 copy-done.3
  46.8 0.4 shard_map.133
  47.1 8.9 %all_to_all.22.rows_ref = bf16[8,4,3584]{2,1,0:T(4,128)(2,1)S(1)} all-to-all(bf16[8,4,3584]{2,1,0:T(4,128)(2,1)S(1)} %get-tuple-element.30), channel_id=1, replica_groups={{0,2,4,6,8,10,12,14},{16,18,20,22,24,26,28,30},{1,3,5,7,9,11,13,15},{17..., dimensions={0} | all-to-all | bytes 458752 | tf_op jit(solution)/shard_map/all_to_all | solution.py:617
  56.0 0.0 collective-permute-start.2
  56.0 1.5 %shard_map.134 = (bf16[32,512]{1,0:T(8,128)(2,1)S(1)}, bf16[256,3584]{1,0:T(8,128)(2,1)S(1)}) custom-call(bf16[8,4,3584]{2,1,0:T(4,128)(2,1)S(1)} %all_to_all.22.rows_ref, bf16[3584,512]{1,0:T(8,128)(2,1)S(1)} %get-tuple-element.29.ready_ref.gate_ref, bf16[3584,512]{1,0:T(8,128)(2,1)S(1)} %get-tuple-element.31.up_ref, bf16[512,3584]{1,0:T(8,128)(2,1)} %bitcast.11), custom_call_target="tpu_custom_call" | custom-call | flops 234881024 | bytes 9175040 | tf_op jit(solution)/shard_map/pallas_call | solution.py:514
  57.6 0.0 collective-permute-done.2.rows_ref
  57.6 2.0 %shard_map.136 = bf16[32,3584]{1,0:T(8,128)(2,1)S(1)} custom-call(bf16[8,4,3584]{2,1,0:T(4,128)(2,1)S(1)} %collective-permute-done.2.rows_ref, bf16[3584,512]{1,0:T(8,128)(2,1)S(1)} %get-tuple-element.29.ready_ref.gate_ref, bf16[3584,512]{1,0:T(8,128)(2,1)S(1)} %get-tuple-element.31.up_ref, bf16[256,3584]{1,0:T(8,128)(2,1)S(1)} %get-tuple-element.33.top_ref, ...), custom_call_target="tpu_custom_call" | custom-call | tf_op jit(solution)/shard_map/pallas_call | solution.py:539
  59.6 0.5 collective-permute-start.3
  60.2 0.7 shard_map.135.keep_ref
  60.9 0.4 collective-permute-done.3.other_ref
  61.3 0.1 shard_map.137
  61.4 12.6 %all_to_all.23.returned_ref = bf16[16,2,3584]{2,1,0:T(2,128)(2,1)S(1)} all-to-all(bf16[16,2,3584]{2,1,0:T(2,128)(2,1)S(1)} %shard_map.137), channel_id=1, replica_groups=mesh['groups'=1,'ep'=16,'side'=2] {'ep'}, dimensions={0} | all-to-all | bytes 458752 | tf_op jit(solution)/shard_map/all_to_all | solution.py:626
  74.0 0.8 %shard_map.138 = bf16[4,3584]{1,0:T(4,128)(2,1)} custom-call(bf16[16,2,3584]{2,1,0:T(2,128)(2,1)S(1)} %all_to_all.23.returned_ref, f32[4,128]{1,0:T(4,128)S(1)} %get-tuple-element.35.coefficient_ref, f32[4,3584]{1,0:T(4,128)S(1)} %get-tuple-element.36.stream_ref), custom_call_target="tpu_custom_call" | custom-call | tf_op jit(solution)/shard_map/pallas_call | solution.py:467
Async XLA Ops:
  27.0 1.9 %collective-permute-start = (bf16[64,3584]{1,0:T(8,128)(2,1)S(1)}, bf16[64,3584]{1,0:T(8,128)(2,1)S(1)}, u32[]{:S(2)}, u32[]{:S(2)}) collective-permute-start(bf16[64,3584]{1,0:T(8,128)(2,1)S(1)} %get-tuple-element.26), channel_id=1, source_target_pairs={{0,1},{1,0},{2,3},{3,2},{4,5},{5,4},{6,7},{7,6},{8,9},{9,8},{10,11... | collective-permute-start | bytes 1376264 | tf_op jit(solution)/shard_map/ppermute | solution.py:568
  27.1 13.8 %copy-start = (bf16[4,3584]{1,0:T(4,128)(2,1)S(1)}, bf16[4,3584]{1,0:T(4,128)(2,1)}, u32[]{:S(2)}) copy-start(bf16[4,3584]{1,0:T(4,128)(2,1)} %residual_ref.1) | copy-start | bytes 86020
  27.1 13.8 %copy-start.2 = (s32[4,8]{1,0:T(4,128)S(1)}, s32[4,8]{1,0:T(4,128)}, u32[]{:S(2)}) copy-start(s32[4,8]{1,0:T(4,128)} %ids_ref.3) | copy-start | bytes 388
  41.0 5.8 %collective-permute-start.1 = (bf16[8,3712]{1,0:T(8,128)(2,1)S(1)}, bf16[8,3712]{1,0:T(8,128)(2,1)S(1)}, u32[]{:S(2)}, u32[]{:S(2)}) collective-permute-start(bf16[8,3712]{1,0:T(8,128)(2,1)S(1)} %get-tuple-element.28.after_ref), channel_id=1, source_target_pairs={{0,16},{2,18},{4,20},{6,22},{8,24},{10,26},{12,28},{14,30},{16,0},... | collective-permute-start | bytes 178184 | tf_op jit(solution)/shard_map/ppermute | solution.py:610
  42.4 4.3 %copy-start.1 = (f32[3584]{0:T(1024)S(1)}, f32[3584]{0:T(1024)}, u32[]{:S(2)}) copy-start(f32[3584]{0:T(1024)} %param.18) | copy-start | bytes 43012
  42.4 4.3 %copy-start.3 = (f32[4,8]{1,0:T(4,128)S(1)}, f32[4,8]{1,0:T(4,128)}, u32[]{:S(2)}) copy-start(f32[4,8]{1,0:T(4,128)} %share_ref.1) | copy-start | bytes 388
  56.0 1.5 %collective-permute-start.2 = (bf16[8,4,3584]{2,1,0:T(4,128)(2,1)S(1)}, bf16[8,4,3584]{2,1,0:T(4,128)(2,1)S(1)}, u32[]{:S(2)}, u32[]{:S(2)}) collective-permute-start(bf16[8,4,3584]{2,1,0:T(4,128)(2,1)S(1)} %all_to_all.22.rows_ref), channel_id=1, source_target_pairs={{0,1},{1,0},{2,3},{3,2},{4,5},{5,4},{6,7},{7,6},{8,9},{9,8},{10,11... | collective-permute-start | bytes 688136 | tf_op jit(solution)/shard_map/ppermute | solution.py:568
  59.6 1.6 %collective-permute-start.3 = (bf16[32,3584]{1,0:T(8,128)(2,1)S(1)}, bf16[32,3584]{1,0:T(8,128)(2,1)S(1)}, u32[]{:S(2)}, u32[]{:S(2)}) collective-permute-start(bf16[32,3584]{1,0:T(8,128)(2,1)S(1)} %shard_map.136), channel_id=1, source_target_pairs={{0,1},{1,0},{2,3},{3,2},{4,5},{5,4},{6,7},{7,6},{8,9},{9,8},{10,11... | collective-permute-start | bytes 688136 | tf_op jit(solution)/shard_map/ppermute | solution.py:568

commit v6 on v5

--- a/solution.py
+++ b/solution.py
@@ -184,7 +184,11 @@
     own_heads, _, value_width = up_ref.shape
     rows = sources * tokens_in
     latent = arrived_ref[...].reshape(sources * block, latent_width)
-    head = lax.broadcasted_iota(jnp.int32, (sources * block, value_width), 0) % own_heads
+    if 8 % own_heads == 0 and sources * block % 8 == 0:
+        head = lax.rem(lax.broadcasted_iota(jnp.int32, (8, value_width), 0), own_heads)
+        head = jnp.concatenate([head] * (sources * block // 8), axis=0)
+    else:
+        head = lax.broadcasted_iota(jnp.int32, (sources * block, value_width), 0) % own_heads
     outs = []
     for i in range(own_heads):
         out = jnp.dot(latent, up_ref[i], preferred_element_type=jnp.float32)
@@ -192,14 +196,16 @@
     heads = jnp.concatenate(outs, axis=1)
     side = lax.axis_index("side")
     half = rows // 2
-    target = lax.broadcasted_iota(jnp.int32, (rows, rows * own_heads), 0)
-    source = lax.broadcasted_iota(jnp.int32, (rows, rows * own_heads), 1) // own_heads
+    target = lax.broadcasted_iota(jnp.int32, (rows, LANES), 0)
+    source = lax.broadcasted_iota(jnp.int32, (8, rows * own_heads), 1) // own_heads
+    source = jnp.concatenate([source] * (rows // 8), axis=0)
     within = jnp.where(target < half, target, target - half)
     wanted_side = jnp.where(target < half, side, 1 - side)
     zone = (within // tokens_in) % 2
     member = within // (2 * tokens_in)
     chip = zone * (half // (2 * tokens_in)) + member
     origin = chip * (2 * tokens_in) + wanted_side * tokens_in + within % tokens_in
+    origin = jnp.concatenate([origin] * (rows * own_heads // LANES), axis=1)
     sorter = jnp.where(source == origin, 1.0, 0.0).astype(jnp.bfloat16)
     ordered = jnp.dot(sorter, heads, preferred_element_type=jnp.float32).astype(jnp.bfloat16)
     own_ref[...] = ordered[:half]

time: 75.1 us -> 75.5 us (level)
  no operation moved by 1% of the time
where the time goes in v6:
time: 75.5 us; the launch traced here: 75.2 us
  blocking collectives  56.2 us (74%)
  Pallas kernels  14.8 us (20%)
  starting transfers between devices  2.08 us (3%)
  waiting for transfers between devices  2.03 us (3%)
    all_to_all x1, blocking collectives, local(): lax.all_to_all(latent, ('ep', 'side'), split_axis=0, concat_axis=0, tiled...  22.7 us
    all_to_all x1, blocking collectives, local(): lax.all_to_all(both, 'ep', split_axis=0, concat_axis=0, tiled=True)  12.6 us
    all_to_all x1, blocking collectives, local(): lax.all_to_all(contribution, 'ep', split_axis=0, concat_axis=0, tiled=Tru...  11.9 us
    all_to_all x1, blocking collectives, local(): lax.all_to_all(outbound, 'ep', split_axis=0, concat_axis=0, tiled=True, a...  8.9 us
    pallas_call x1, Pallas kernels, load_weights(): pl.pallas_call(load_kernel, out_shape=[pltpu.VMEM(gate.shape, gate.dtype)...  3.7 us
    pallas_call x1, Pallas kernels, attend(): pl.pallas_call(attention_kernel, out_shape=[jax.ShapeDtypeStruct((holders...  2.54 us
    pallas_call x1, Pallas kernels, project_heads(): pl.pallas_call(head_kernel, out_shape=[jax.ShapeDtypeStruct((half, featur...  2.08 us
    pallas_call x1, Pallas kernels, other_partial(): pl.pallas_call(other_partial_kernel, out_shape=jax.ShapeDtypeStruct((coun...  2.04 us
  transfers between devices with their start and end apart: 4, of which 3 were waited for; matrix products, arithmetic and copies ran while one was open for 0% of the time, Pallas kernels for 9%

profile of v6, /device:TPU:0, one launch (start us, length us, event | category | flops | bytes accessed | tf_op | source)
XLA Modules:
  0.0 75.2 jit_solution(9624021760428304935)
XLA Ops:
  0.0 2.5 %shard_map.127 = (bf16[32,16,512]{2,1,0:T(8,128)(2,1)S(1)}, bf16[4,512,128]{2,1,0:T(8,128)(2,1)S(1)}, bf16[512,2560]{1,0:T(8,128)(2,1)S(1)}) custom-call(s32[2]{0:T(128)} %lengths_hbm.1, bf16[4,576,128]{2,1,0:T(8,128)(2,1)} %bitcast.14, bf16[2,576,128]{2,1,0:T(8,128)(2,1)} %bitcast.15, bf16[4,576]{1,0:T(4,128)(2,1)} %fresh_hbm.1, ...), custom_call_target="tpu_custom_call" | custom-call | tf_op jit(solution)/shard_map/pallas_call | solution.py:153
  2.5 22.7 %all_to_all.20.arrived_ref = bf16[32,16,512]{2,1,0:T(8,128)(2,1)S(1)} all-to-all(bf16[32,16,512]{2,1,0:T(8,128)(2,1)S(1)} %get-tuple-element.21), channel_id=1, replica_groups=mesh['groups'=1,'ep'=16,'side'=2] {'ep','side'}, dimensions={0} | all-to-all | bytes 1048576 | tf_op jit(solution)/shard_map/all_to_all | solution.py:605
  25.3 2.1 %shard_map.128 = (bf16[64,3584]{1,0:T(8,128)(2,1)S(1)}, bf16[64,512]{1,0:T(8,128)(2,1)S(1)}, bf16[512,1024]{1,0:T(8,128)(2,1)S(1)}) custom-call(bf16[32,16,512]{2,1,0:T(8,128)(2,1)S(1)} %all_to_all.20.arrived_ref, bf16[4,512,128]{2,1,0:T(8,128)(2,1)S(1)} %get-tuple-element.22.up_ref, bf16[512,2560]{1,0:T(8,128)(2,1)S(1)} %get-tuple-element.23.left_ref, ...), custom_call_target="tpu_custom_call" | custom-call | tf_op jit(solution)/shard_map/pallas_call | solution.py:223
  27.4 0.1 collective-permute-start
  27.5 0.0 copy-start
  27.5 0.0 copy-start.2
  27.5 0.7 shard_map.129.keep_ref
  28.2 1.0 %collective-permute-done.other_ref = bf16[64,3584]{1,0:T(8,128)(2,1)S(1)} collective-permute-done((bf16[64,3584]{1,0:T(8,128)(2,1)S(1)}, bf16[64,3584]{1,0:T(8,128)(2,1)S(1)}, u32[]{:S(2)}, u32[]{:S(2)}) %collective-permute-start) | collective-permute-done | bytes 458784 | tf_op jit(solution)/shard_map/ppermute | solution.py:574
  29.3 0.1 shard_map.130
  29.3 11.9 %all_to_all.21.shared_ref = bf16[8,8,3584]{2,1,0:T(8,128)(2,1)S(1)} all-to-all(bf16[8,8,3584]{2,1,0:T(8,128)(2,1)S(1)} %shard_map.130), channel_id=1, replica_groups={{0,2,4,6,8,10,12,14},{16,18,20,22,24,26,28,30},{1,3,5,7,9,11,13,15},{17..., dimensions={0} | all-to-all | bytes 917504 | tf_op jit(solution)/shard_map/all_to_all | solution.py:612
  41.3 0.0 copy-done
  41.3 0.0 copy-done.2
  41.3 0.1 shard_map.131
  41.4 1.5 %collective-permute-start.1 = (bf16[8,3712]{1,0:T(8,128)(2,1)S(1)}, bf16[8,3712]{1,0:T(8,128)(2,1)S(1)}, u32[]{:S(2)}, u32[]{:S(2)}) collective-permute-start(bf16[8,3712]{1,0:T(8,128)(2,1)S(1)} %get-tuple-element.28.after_ref), channel_id=1, source_target_pairs={{0,16},{2,18},{4,20},{6,22},{8,24},{10,26},{12,28},{14,30},{16,0},... | collective-permute-start | bytes 178184 | tf_op jit(solution)/shard_map/ppermute | solution.py:616
  42.9 0.0 copy-start.1
  42.9 0.0 copy-start.3
  42.9 3.7 %shard_map.132 = (bf16[3584,512]{1,0:T(8,128)(2,1)S(1)}, bf16[3584,512]{1,0:T(8,128)(2,1)S(1)}, bf16[256,3584]{1,0:T(8,128)(2,1)S(1)}) custom-call(bf16[8,3712]{1,0:T(8,128)(2,1)S(1)} %get-tuple-element.28.after_ref, bf16[3584,512]{1,0:T(8,128)(2,1)} %bitcast.12, bf16[3584,512]{1,0:T(8,128)(2,1)} %bitcast.13, bf16[512,3584]{1,0:T(8,128)(2,1)} %bitcast.10), custom_call_target="tpu_custom_call" | custom-call | bytes 9175040 | tf_op jit(solution)/shard_map/pallas_call | solution.py:272
  46.6 0.6 collective-permute-done.1.other_ref
  47.2 0.0 copy-done.1
  47.2 0.0 copy-done.3
  47.2 0.4 shard_map.133
  47.6 8.9 %all_to_all.22.rows_ref = bf16[8,4,3584]{2,1,0:T(4,128)(2,1)S(1)} all-to-all(bf16[8,4,3584]{2,1,0:T(4,128)(2,1)S(1)} %get-tuple-element.30), channel_id=1, replica_groups={{0,2,4,6,8,10,12,14},{16,18,20,22,24,26,28,30},{1,3,5,7,9,11,13,15},{17..., dimensions={0} | all-to-all | bytes 458752 | tf_op jit(solution)/shard_map/all_to_all | solution.py:623
  56.4 0.0 collective-permute-start.2
  56.5 1.5 %shard_map.134 = (bf16[32,512]{1,0:T(8,128)(2,1)S(1)}, bf16[256,3584]{1,0:T(8,128)(2,1)S(1)}) custom-call(bf16[8,4,3584]{2,1,0:T(4,128)(2,1)S(1)} %all_to_all.22.rows_ref, bf16[3584,512]{1,0:T(8,128)(2,1)S(1)} %get-tuple-element.29.ready_ref.gate_ref, bf16[3584,512]{1,0:T(8,128)(2,1)S(1)} %get-tuple-element.31.up_ref, bf16[512,3584]{1,0:T(8,128)(2,1)} %bitcast.11), custom_call_target="tpu_custom_call" | custom-call | flops 234881024 | bytes 9175040 | tf_op jit(solution)/shard_map/pallas_call | solution.py:520
  58.0 0.0 collective-permute-done.2.rows_ref
  58.0 2.0 %shard_map.136 = bf16[32,3584]{1,0:T(8,128)(2,1)S(1)} custom-call(bf16[8,4,3584]{2,1,0:T(4,128)(2,1)S(1)} %collective-permute-done.2.rows_ref, bf16[3584,512]{1,0:T(8,128)(2,1)S(1)} %get-tuple-element.29.ready_ref.gate_ref, bf16[3584,512]{1,0:T(8,128)(2,1)S(1)} %get-tuple-element.31.up_ref, bf16[256,3584]{1,0:T(8,128)(2,1)S(1)} %get-tuple-element.33.top_ref, ...), custom_call_target="tpu_custom_call" | custom-call | tf_op jit(solution)/shard_map/pallas_call | solution.py:545
  60.0 0.5 collective-permute-start.3
  60.6 0.7 shard_map.135.keep_ref
  61.3 0.4 collective-permute-done.3.other_ref
  61.7 0.1 shard_map.137
  61.8 12.6 %all_to_all.23.returned_ref = bf16[16,2,3584]{2,1,0:T(2,128)(2,1)S(1)} all-to-all(bf16[16,2,3584]{2,1,0:T(2,128)(2,1)S(1)} %shard_map.137), channel_id=1, replica_groups=mesh['groups'=1,'ep'=16,'side'=2] {'ep'}, dimensions={0} | all-to-all | bytes 458752 | tf_op jit(solution)/shard_map/all_to_all | solution.py:632
  74.4 0.8 %shard_map.138 = bf16[4,3584]{1,0:T(4,128)(2,1)} custom-call(bf16[16,2,3584]{2,1,0:T(2,128)(2,1)S(1)} %all_to_all.23.returned_ref, f32[4,128]{1,0:T(4,128)S(1)} %get-tuple-element.35.coefficient_ref, f32[4,3584]{1,0:T(4,128)S(1)} %get-tuple-element.36.stream_ref), custom_call_target="tpu_custom_call" | custom-call | tf_op jit(solution)/shard_map/pallas_call | solution.py:473
Async XLA Ops:
  27.4 1.9 %collective-permute-start = (bf16[64,3584]{1,0:T(8,128)(2,1)S(1)}, bf16[64,3584]{1,0:T(8,128)(2,1)S(1)}, u32[]{:S(2)}, u32[]{:S(2)}) collective-permute-start(bf16[64,3584]{1,0:T(8,128)(2,1)S(1)} %get-tuple-element.26), channel_id=1, source_target_pairs={{0,1},{1,0},{2,3},{3,2},{4,5},{5,4},{6,7},{7,6},{8,9},{9,8},{10,11... | collective-permute-start | bytes 1376264 | tf_op jit(solution)/shard_map/ppermute | solution.py:574
  27.5 13.8 %copy-start = (bf16[4,3584]{1,0:T(4,128)(2,1)S(1)}, bf16[4,3584]{1,0:T(4,128)(2,1)}, u32[]{:S(2)}) copy-start(bf16[4,3584]{1,0:T(4,128)(2,1)} %residual_ref.1) | copy-start | bytes 86020
  27.5 13.8 %copy-start.2 = (s32[4,8]{1,0:T(4,128)S(1)}, s32[4,8]{1,0:T(4,128)}, u32[]{:S(2)}) copy-start(s32[4,8]{1,0:T(4,128)} %ids_ref.3) | copy-start | bytes 388
  41.4 5.8 %collective-permute-start.1 = (bf16[8,3712]{1,0:T(8,128)(2,1)S(1)}, bf16[8,3712]{1,0:T(8,128)(2,1)S(1)}, u32[]{:S(2)}, u32[]{:S(2)}) collective-permute-start(bf16[8,3712]{1,0:T(8,128)(2,1)S(1)} %get-tuple-element.28.after_ref), channel_id=1, source_target_pairs={{0,16},{2,18},{4,20},{6,22},{8,24},{10,26},{12,28},{14,30},{16,0},... | collective-permute-start | bytes 178184 | tf_op jit(solution)/shard_map/ppermute | solution.py:616
  42.9 4.3 %copy-start.1 = (f32[3584]{0:T(1024)S(1)}, f32[3584]{0:T(1024)}, u32[]{:S(2)}) copy-start(f32[3584]{0:T(1024)} %param.18) | copy-start | bytes 43012
  42.9 4.3 %copy-start.3 = (f32[4,8]{1,0:T(4,128)S(1)}, f32[4,8]{1,0:T(4,128)}, u32[]{:S(2)}) copy-start(f32[4,8]{1,0:T(4,128)} %share_ref.1) | copy-start | bytes 388
  56.4 1.5 %collective-permute-start.2 = (bf16[8,4,3584]{2,1,0:T(4,128)(2,1)S(1)}, bf16[8,4,3584]{2,1,0:T(4,128)(2,1)S(1)}, u32[]{:S(2)}, u32[]{:S(2)}) collective-permute-start(bf16[8,4,3584]{2,1,0:T(4,128)(2,1)S(1)} %all_to_all.22.rows_ref), channel_id=1, source_target_pairs={{0,1},{1,0},{2,3},{3,2},{4,5},{5,4},{6,7},{7,6},{8,9},{9,8},{10,11... | collective-permute-start | bytes 688136 | tf_op jit(solution)/shard_map/ppermute | solution.py:574
  60.0 1.6 %collective-permute-start.3 = (bf16[32,3584]{1,0:T(8,128)(2,1)S(1)}, bf16[32,3584]{1,0:T(8,128)(2,1)S(1)}, u32[]{:S(2)}, u32[]{:S(2)}) collective-permute-start(bf16[32,3584]{1,0:T(8,128)(2,1)S(1)} %shard_map.136), channel_id=1, source_target_pairs={{0,1},{1,0},{2,3},{3,2},{4,5},{5,4},{6,7},{7,6},{8,9},{9,8},{10,11... | collective-permute-start | bytes 688136 | tf_op jit(solution)/shard_map/ppermute | solution.py:574
